TPU v7x, 32 devices: a whole 2x2x4 slice. The times are simulated.
32 devices in a mesh: gx: 4 (over y, x), gy: 8 (over z, core).
Axes of the slice: x: 2, y: 2, z: 4, core: 2. Of those that a mesh axis runs over, the one named last changes fastest.
Arguments:
- fields: float32 [4, 128, 64, 1024], P(None, None, 'gx', 'gy'), may hold values from -6 to 6
- courant: float32 [2, 128, 64, 1024], P(None, None, 'gx', 'gy'), may hold values from -0.3 to 0.3
- sun_columns: int32 [4, 8, 2048], P('gx', 'gy'), may hold values from -1 to 2047, as said below
- rad_w1: bfloat16 [512, 1024], replicated, may hold values from -0.25 to 0.25
- rad_b1: float32 [1024], replicated, may hold values from -3 to 3
- rad_w2: bfloat16 [1024, 1024], replicated, may hold values from -0.1875 to 0.1875
- rad_b2: float32 [1024], replicated, may hold values from -3 to 3
- rad_w3: bfloat16 [1024, 512], replicated, may hold values from -0.1875 to 0.1875
- segment_route: int32 [2, 4, 8, 1024], P(None, 'gx', 'gy'), may hold values from 0 to 1023, as said below
- regrid_weights: bfloat16 [4, 8, 16, 128, 128], P('gx', 'gy'), may hold values from 0 to 1, as said below
- chem_w1: bfloat16 [256, 1024], replicated, may hold values from -0.375 to 0.375
- chem_b1: float32 [1024], replicated, may hold values from -3 to 3
- chem_w2: bfloat16 [1024, 256], replicated, may hold values from -0.1875 to 0.1875
Outputs:
- fields_out: float32 [4, 128, 64, 1024], P(None, None, 'gx', 'gy')
- chem_tendency: bfloat16 [4, 8, 2048, 256], P('gx', 'gy')
Inputs may be any that keep to these rules, and one draw needn't show every extreme that they name: `sun_columns`: in each tile the live entries come first and are distinct columns of the tile; the rest are -1. Counting a tile's sunlit blocks as its live entries divided by 128, rounded up, a tile and the tile with the same first index and second index 4 further (modulo 8) have exactly 16 sunlit blocks together. `segment_route`: entry 0 is the receiving tile, entry 1 the slot there. Every tile receives exactly 1024 segments, one in each slot; no tile receives more than 64 segments from one tile, and some tile receives exactly 64 from one tile. `regrid_weights`: entries are nonnegative and each row sums to one up to rounding.
All inputs are finite; a program needn't handle non-finite values.
Results may differ from a plain program's by a relative error of at most 0.0075.
Values may be sent and summed in bfloat16 or wider, within the bound.
A program may use at most 128 MiB of HBM per device.

v0:
```python
import jax
import jax.numpy as jnp
from jax import lax
from jax.sharding import PartitionSpec as P

BLOCK = 128
SEG = 2
STEPS = 2


def padded(block, sides, width, periodic):
    for axis, dim in sides:
        count = lax.axis_size(axis)
        forward = [(i, i + 1) for i in range(count - 1)]
        if periodic:
            forward.append((count - 1, 0))
        backward = [(target, source) for source, target in forward]
        low = lax.ppermute(
            lax.slice_in_dim(block, block.shape[dim] - width, None, axis=dim), axis, forward
        )
        high = lax.ppermute(lax.slice_in_dim(block, 0, width, axis=dim), axis, backward)
        block = jnp.concatenate([low, block, high], axis=dim)
    return block


def advect(fields, courant):
    field_count, levels, tile_rows, tile_cols = fields.shape
    lat_pack = jnp.concatenate([fields, courant[0:1]], axis=0)
    lon_pack = jnp.concatenate([fields, courant[1:2]], axis=0)
    lat_rim = padded(lat_pack, (("gx", 2),), 1, False)
    lon_rim = padded(lon_pack, (("gy", 3),), 1, True)
    total_rows = tile_rows * lax.axis_size("gx")
    lower_row = lax.axis_index("gx") * tile_rows - 1 + jnp.arange(tile_rows + 1)
    valid_face = ((lower_row >= 0) & (lower_row <= total_rows - 2)).astype(jnp.float32)
    cells_lat = lat_rim[:field_count]
    speed_lat = lat_rim[field_count]
    face_lat = 0.5 * (speed_lat[:, :-1] + speed_lat[:, 1:]) * valid_face[None, :, None]
    flux_lat = (
        jnp.maximum(face_lat, 0.0) * cells_lat[:, :, :-1]
        + jnp.minimum(face_lat, 0.0) * cells_lat[:, :, 1:]
    )
    cells_lon = lon_rim[:field_count]
    speed_lon = lon_rim[field_count]
    face_lon = 0.5 * (speed_lon[:, :, :-1] + speed_lon[:, :, 1:])
    flux_lon = (
        jnp.maximum(face_lon, 0.0) * cells_lon[..., :-1]
        + jnp.minimum(face_lon, 0.0) * cells_lon[..., 1:]
    )
    return (
        fields
        - (flux_lat[:, :, 1:] - flux_lat[:, :, :-1])
        - (flux_lon[..., 1:] - flux_lon[..., :-1])
    )


def radiation_net(features, rad_w1, rad_b1, rad_w2, rad_b2, rad_w3):
    contract = (((0,), (0,)), ((), ()))
    layer_one = jax.nn.silu(
        lax.dot_general(rad_w1, features, contract, preferred_element_type=jnp.float32)
        + rad_b1[:, None]
    ).astype(jnp.bfloat16)
    layer_two = jax.nn.silu(
        lax.dot_general(rad_w2, layer_one, contract, preferred_element_type=jnp.float32)
        + rad_b2[:, None]
    ).astype(jnp.bfloat16)
    return lax.dot_general(rad_w3, layer_two, contract, preferred_element_type=jnp.float32)


def radiate(fields, sun_columns, rad_w1, rad_b1, rad_w2, rad_b2, rad_w3):
    field_count, levels, tile_rows, tile_cols = fields.shape
    flat_fields = fields.reshape(field_count * levels, tile_rows * tile_cols)
    slot_list = sun_columns.reshape(-1)
    lit_mask = slot_list >= 0
    safe_index = jnp.where(lit_mask, slot_list, 0)
    features = (jnp.take(flat_fields, safe_index, axis=1) * lit_mask[None, :]).astype(jnp.bfloat16)
    heating = radiation_net(features, rad_w1, rad_b1, rad_w2, rad_b2, rad_w3)
    tendency = (
        jnp.zeros_like(flat_fields)
        .at[:, safe_index]
        .add(jnp.where(lit_mask[None, :], heating, 0.0))
    )
    return fields + tendency.reshape(fields.shape)


def chemistry(fields, segment_route, regrid_weights, chem_w1, chem_b1, chem_w2):
    field_count, levels, tile_rows, tile_cols = fields.shape
    columns = tile_rows * tile_cols
    segment_count = columns // SEG
    tile_count = lax.axis_size("gx") * lax.axis_size("gy")
    capacity = max(2, 2 * segment_count // tile_count)
    source = fields[2:4].astype(jnp.bfloat16).reshape(2 * levels, segment_count, SEG)
    destination = segment_route[0].reshape(-1)
    arrival_slot = segment_route[1].reshape(-1)
    segment_index = jnp.arange(segment_count)
    same_target = (destination[None, :] == destination[:, None]) & (
        segment_index[None, :] < segment_index[:, None]
    )
    order_rank = jnp.sum(same_target.astype(jnp.int32), axis=1)
    target_row = destination * capacity + order_rank
    placement = target_row[None, :] == jnp.arange(tile_count * capacity)[:, None]
    packed = jnp.einsum(
        "ps,fsc->pcf", placement.astype(jnp.bfloat16), source, preferred_element_type=jnp.float32
    ).astype(jnp.bfloat16)
    slot_tags = jnp.sum(jnp.where(placement, arrival_slot[None, :] + 1, 0), axis=1) - 1
    packed = packed.reshape(tile_count, capacity, SEG * 2 * levels)
    slot_tags = slot_tags.reshape(tile_count, capacity)
    arrived, arrived_tags = (
        lax.all_to_all(packed, ("gx", "gy"), split_axis=0, concat_axis=0, tiled=True),
        lax.all_to_all(slot_tags, ("gx", "gy"), split_axis=0, concat_axis=0, tiled=True),
    )
    arrived = arrived.reshape(tile_count * capacity, SEG * 2 * levels)
    arrived_tags = arrived_tags.reshape(-1)
    selector = (arrived_tags[None, :] == segment_index[:, None]).astype(jnp.bfloat16)
    placed = jnp.dot(selector, arrived, preferred_element_type=jnp.float32).astype(jnp.bfloat16)
    block_count = columns // BLOCK
    chem_cells = placed.reshape(block_count, BLOCK, 2 * levels)
    regridded = jnp.einsum(
        "jab,jbf->jaf", regrid_weights[0, 0], chem_cells, preferred_element_type=jnp.float32
    ).astype(jnp.bfloat16)
    flat_cells = regridded.reshape(columns, 2 * levels)
    chem_hidden = jax.nn.silu(
        jnp.dot(flat_cells, chem_w1, preferred_element_type=jnp.float32) + chem_b1
    ).astype(jnp.bfloat16)
    output = jnp.dot(chem_hidden, chem_w2, preferred_element_type=jnp.float32).astype(jnp.bfloat16)
    return output.reshape(1, 1, columns, 2 * levels)


def local(
    fields,
    courant,
    sun_columns,
    rad_w1,
    rad_b1,
    rad_w2,
    rad_b2,
    rad_w3,
    segment_route,
    regrid_weights,
    chem_w1,
    chem_b1,
    chem_w2,
):
    current = fields
    for repeat in range(STEPS):
        current = advect(current, courant)
        current = radiate(current, sun_columns, rad_w1, rad_b1, rad_w2, rad_b2, rad_w3)
    chem_output = chemistry(current, segment_route, regrid_weights, chem_w1, chem_b1, chem_w2)
    return (current, chem_output)


def solution(mesh):
    return jax.shard_map(
        local,
        mesh=mesh,
        in_specs=(
            P(None, None, "gx", "gy"),
            P(None, None, "gx", "gy"),
            P("gx", "gy", None),
            P(),
            P(),
            P(),
            P(),
            P(),
            P(None, "gx", "gy", None),
            P("gx", "gy", None, None, None),
            P(),
            P(),
            P(),
        ),
        out_specs=(P(None, None, "gx", "gy"), P("gx", "gy", None, None)),
        check_vma=False,
    )
```

profile of v0, /device:TPU:0, one launch (start us, length us, event | category | flops | bytes accessed | tf_op | source)
XLA Modules:
  0.0 304.2 jit_solution(1587831249233824712)
XLA Ops:
  0.6 5.9 %copy.41 = f32[4,128,16,128]{1,2,3,0:T(8,128)} copy(f32[4,128,16,128]{3,2,1,0:T(8,128)} %param.15) | data formatting | bytes 8388608 | tf_op args[0]
  15.1 5.6 %collective-permute-start = (f32[5,128,1,128]{1,2,3,0:T(1,128)}, f32[5,128,1,128]{1,2,3,0:T(1,128)}, u32[]{:S(2)}, u32[]{:S(2)}) collective-permute-start(f32[5,128,1,128]{1,2,3,0:T(1,128)} %get-tuple-element.19), channel_id=1, source_target_pairs={{0,8},{8,16},{16,24},{1,9},{9,17},{17,25},{2,10},{10,18},{18,26},{... | collective-permute-start | bytes 983048 | tf_op jit(solution)/shard_map/ppermute | solution.py:18
  34.4 5.6 %all-to-all-start = ((s32[32,1,64]{2,1,0:T(1,128)}), s32[32,1,64]{2,1,0:T(1,128)}, u32[]{:S(2)}, u32[]{:S(2)}) async-start(s32[32,1,64]{2,1,0:T(1,128)} %sub.44), calls=%async_computation | async-start | bytes 32768 | tf_op jit(solution)/shard_map/all_to_all | solution.py:109
  61.9 12.4 %gather_fusion = f32[2048,512]{1,0:T(8,128)} fusion(f32[512,2048]{0,1:T(8,128)} %bitcast.132, s32[2048]{0:T(1024)} %fusion.113), kind=kCustom, calls=%fused_computation.clone | custom fusion | bytes 8396800 | tf_op jit(solution)/shard_map/jit(_take)/gather | solution.py:75
  74.4 11.1 %fusion.54 = f32[2048,1024]{1,0:T(8,128)} fusion(bf16[1024,1024]{1,0:T(8,128)(2,1)S(1)} %copy-done, f32[1024]{0:T(1024)} %param.19, bf16[512,1024]{1,0:T(8,128)(2,1)} %param.18, f32[2048,512]{1,0:T(8,128)} %gather_fusion, f32[2048]{0:T(1024)} %convert_element_type.60, pred[2048]{0:T(1024)(128)(4,1)} %get-tuple-element.7), kind=kOutput, calls=%fused_computation.94 | convolution fusion | flops 6458179584 | bytes 15742976 | tf_op jit(solution)/shard_map/dot_general | solution.py:63
  85.5 8.1 %fusion.59 = f32[2048,512]{1,0:T(8,128)} fusion(bf16[1024,512]{1,0:T(8,128)(2,1)} %param.22, f32[2048,1024]{1,0:T(8,128)} %fusion.54, f32[1024]{0:T(1024)} %param.21), kind=kOutput, calls=%fused_computation.97 | convolution fusion | flops 2160066560 | bytes 13635584 | tf_op jit(solution)/shard_map/dot_general | solution.py:66
  93.6 17.0 %scatter_custom_fusion = f32[512,2048]{0,1:T(8,128)} fusion(s32[2048]{0:T(1024)} %bitcast.140, f32[2048,512]{1,0:T(8,128)} %fusion.59, f32[]{:T(128)} %constant.11.clone.1, pred[2048]{0:T(1024)(128)(4,1)} %copy-done.8), kind=kCustom, calls=%fused_computation.91 | custom fusion | flops 2097152 | bytes 8391680 | tf_op jit(solution)/shard_map/scatter-add | solution.py:80
  110.6 5.3 %reshape.142 = f32[4,128,16,128]{1,0,3,2:T(4,128)} reshape(f32[512,2048]{0,1:T(8,128)} %scatter_custom_fusion) | data formatting | bytes 8388608 | tf_op jit(solution)/shard_map/reshape | solution.py:82
  115.9 5.9 %copy_add_fusion.1 = f32[4,128,16,128]{1,2,3,0:T(8,128)S(1)} fusion(f32[4,128,16,128]{1,2,3,0:T(8,128)} %copy-done.5, f32[4,128,16,128]{1,0,3,2:T(4,128)} %reshape.142), kind=kLoop, calls=%fused_computation.84 | loop fusion | flops 1048576 | bytes 12582912 | tf_op jit(solution)/shard_map/add | solution.py:82
  126.2 5.9 %collective-permute-start.4 = (f32[5,128,1,128]{1,2,3,0:T(1,128)S(1)}, f32[5,128,1,128]{1,2,3,0:T(1,128)S(1)}, u32[]{:S(2)}, u32[]{:S(2)}) collective-permute-start(f32[5,128,1,128]{1,2,3,0:T(1,128)S(1)} %get-tuple-element.15), channel_id=1, source_target_pairs={{0,8},{8,16},{16,24},{1,9},{9,17},{17,25},{2,10},{10,18},{18,26},{... | collective-permute-start | bytes 983048 | tf_op jit(solution)/shard_map/ppermute | solution.py:18
  136.6 8.0 %collective-permute-done.5 = f32[5,128,1,128]{1,2,3,0:T(1,128)S(1)} collective-permute-done((f32[5,128,1,128]{1,2,3,0:T(1,128)S(1)}, f32[5,128,1,128]{1,2,3,0:T(1,128)S(1)}, u32[]{:S(2)}, u32[]{:S(2)}) %collective-permute-start.5) | collective-permute-done | bytes 327712 | tf_op jit(solution)/shard_map/ppermute | solution.py:21
  153.9 11.7 %gather_fusion.1 = f32[2048,512]{1,0:T(8,128)} fusion(f32[512,2048]{0,1:T(8,128)} %bitcast.131, s32[2048]{0:T(1024)S(1)} %copy-done.7), kind=kCustom, calls=%fused_computation.1.clone | custom fusion | bytes 8396800 | tf_op jit(solution)/shard_map/jit(_take)/gather | solution.py:75
  165.7 11.1 %fusion.52 = f32[2048,1024]{1,0:T(8,128)} fusion(bf16[1024,1024]{1,0:T(8,128)(2,1)S(1)} %copy-done, f32[1024]{0:T(1024)S(1)} %copy-done.16, bf16[512,1024]{1,0:T(8,128)(2,1)} %param.18, f32[2048,512]{1,0:T(8,128)} %gather_fusion.1, f32[2048]{0:T(1024)S(1)} %copy-done.10, pred[2048]{0:T(1024)(128)(4,1)S(1)} %copy-done.15), kind=kOutput, calls=%fused_computation.93 | convolution fusion | flops 6458179584 | bytes 15742976 | tf_op jit(solution)/shard_map/dot_general | solution.py:63
  176.8 8.1 %fusion.57 = f32[2048,512]{1,0:T(8,128)} fusion(bf16[1024,512]{1,0:T(8,128)(2,1)} %param.22, f32[2048,1024]{1,0:T(8,128)} %fusion.52, f32[1024]{0:T(1024)S(1)} %copy-done.17), kind=kOutput, calls=%fused_computation.96 | convolution fusion | flops 2160066560 | bytes 13635584 | tf_op jit(solution)/shard_map/dot_general | solution.py:66
  184.8 16.8 %scatter_custom_fusion.1 = f32[512,2048]{0,1:T(8,128)} fusion(s32[2048]{0:T(1024)} %bitcast.141, f32[2048,512]{1,0:T(8,128)} %fusion.57, f32[]{:T(128)} %constant.11.clone.1, pred[2048]{0:T(1024)(128)(4,1)S(1)} %copy-done.9), kind=kCustom, calls=%fused_computation.89 | custom fusion | flops 2097152 | bytes 8391680 | tf_op jit(solution)/shard_map/scatter-add | solution.py:80
  201.7 5.3 %reshape.144 = f32[4,128,16,128]{1,0,3,2:T(4,128)} reshape(f32[512,2048]{0,1:T(8,128)} %scatter_custom_fusion.1) | data formatting | bytes 8388608 | tf_op jit(solution)/shard_map/reshape | solution.py:82
  207.0 5.9 %copy_add_fusion = f32[4,128,16,128]{1,2,3,0:T(8,128)S(1)} fusion(f32[4,128,16,128]{1,2,3,0:T(8,128)} %copy-done.4, f32[4,128,16,128]{1,0,3,2:T(4,128)} %reshape.144), kind=kLoop, calls=%fused_computation.83 | loop fusion | flops 1048576 | bytes 12582912 | tf_op jit(solution)/shard_map/add | solution.py:82
  217.6 5.1 %fusion.64 = bf16[2048,2,256]{0,2,1:T(8,128)(2,1)} fusion(s32[1024]{0:T(1024)S(1)} %copy-done.12, bf16[256,1024,2]{0,2,1:T(2,128)(2,1)} %reshape.145), kind=kOutput, calls=%fused_computation.99 | convolution fusion | flops 2150629376 | bytes 3149824 | tf_op jit(solution)/shard_map/ps,fsc->pcf/dot_general | solution.py:101
  222.7 6.2 %copy.50 = bf16[2048,2,256]{2,1,0:T(2,128)(2,1)} copy(bf16[2048,2,256]{0,2,1:T(8,128)(2,1)} %fusion.64) | data formatting | bytes 4194304 | tf_op jit(solution)/shard_map/convert_element_type | solution.py:103
  233.2 6.9 %all-to-all-start.1 = ((bf16[32,64,512]{2,1,0:T(8,128)(2,1)}), bf16[32,64,512]{2,1,0:T(8,128)(2,1)}, u32[]{:S(2)}, u32[]{:S(2)}) async-start(bf16[32,64,512]{2,1,0:T(8,128)(2,1)} %reshape.146), calls=%async_computation.1 | async-start | bytes 4194304 | tf_op jit(solution)/shard_map/all_to_all | solution.py:108
  242.2 5.8 %copy.51 = f32[4,128,16,128]{3,2,1,0:T(8,128)} copy(f32[4,128,16,128]{1,2,3,0:T(8,128)} %copy-done.6) | data formatting | bytes 8388608
  247.9 42.2 %all-to-all-done.1 = bf16[32,64,512]{2,1,0:T(8,128)(2,1)} async-done(((bf16[32,64,512]{2,1,0:T(8,128)(2,1)}), bf16[32,64,512]{2,1,0:T(8,128)(2,1)}, u32[]{:S(2)}, u32[]{:S(2)}) %all-to-all-start.1) | async-done | bytes 2097184 | tf_op jit(solution)/shard_map/all_to_all | solution.py:108
  290.2 4.9 %fusion.102 = bf16[1024,512]{1,0:T(8,128)(2,1)} fusion(bf16[2048,512]{1,0:T(8,128)(2,1)} %bitcast.17, s32[2048]{0:T(1024)S(1)} %eq.47), kind=kOutput, calls=%fused_computation.130 | convolution fusion | flops 2150105088 | bytes 3153920 | tf_op jit(solution)/shard_map/dot_general | solution.py:114
  299.0 5.0 %fusion.67 = bf16[1,1,2048,256]{3,2,1,0:T(8,128)(2,1)} fusion(bf16[1024,256]{1,0:T(8,128)(2,1)} %param.27, bf16[2048,256]{1,0:T(8,128)(2,1)} %bitcast.135, bf16[256,1024]{1,0:T(8,128)(2,1)} %param.25, f32[1024]{0:T(1024)S(1)} %copy-done.18), kind=kOutput, calls=%fused_computation.101 | convolution fusion | flops 2160590848 | bytes 3149824 | tf_op jit(solution)/shard_map/dot_general | solution.py:124
  (97 shorter events, 77.0 us)
Async XLA Ops:
  0.6 73.7 %copy-start = (bf16[1024,1024]{1,0:T(8,128)(2,1)S(1)}, bf16[1024,1024]{1,0:T(8,128)(2,1)}, u32[]{:S(2)}) copy-start(bf16[1024,1024]{1,0:T(8,128)(2,1)} %param.20) | copy-start | bytes 6291460
  15.1 35.3 %collective-permute-start = (f32[5,128,1,128]{1,2,3,0:T(1,128)}, f32[5,128,1,128]{1,2,3,0:T(1,128)}, u32[]{:S(2)}, u32[]{:S(2)}) collective-permute-start(f32[5,128,1,128]{1,2,3,0:T(1,128)} %get-tuple-element.19), channel_id=1, source_target_pairs={{0,8},{8,16},{16,24},{1,9},{9,17},{17,25},{2,10},{10,18},{18,26},{... | collective-permute-start | bytes 983048 | tf_op jit(solution)/shard_map/ppermute | solution.py:18
  20.7 29.7 %collective-permute-start.1 = (f32[5,128,1,128]{1,2,3,0:T(1,128)}, f32[5,128,1,128]{1,2,3,0:T(1,128)}, u32[]{:S(2)}, u32[]{:S(2)}) collective-permute-start(f32[5,128,1,128]{1,2,3,0:T(1,128)} %get-tuple-element.9), channel_id=1, source_target_pairs={{8,0},{16,8},{24,16},{9,1},{17,9},{25,17},{10,2},{18,10},{26,18},{... | collective-permute-start | bytes 983048 | tf_op jit(solution)/shard_map/ppermute | solution.py:21
  26.2 19.7 %collective-permute-start.2 = (f32[5,128,16,1]{1,2,3,0:T(8,128)}, f32[5,128,16,1]{1,2,3,0:T(8,128)}, u32[]{:S(2)}, u32[]{:S(2)}) collective-permute-start(f32[5,128,16,1]{1,2,3,0:T(8,128)} %get-tuple-element.11), channel_id=1, source_target_pairs={{0,1},{1,2},{2,3},{3,4},{4,5},{5,6},{6,7},{7,0},{8,9},{9,10},{10,1... | collective-permute-start | bytes 122888 | tf_op jit(solution)/shard_map/ppermute | solution.py:18
  26.2 19.7 %collective-permute-start.3 = (f32[5,128,16,1]{1,2,3,0:T(8,128)}, f32[5,128,16,1]{1,2,3,0:T(8,128)}, u32[]{:S(2)}, u32[]{:S(2)}) collective-permute-start(f32[5,128,16,1]{1,2,3,0:T(8,128)} %get-tuple-element.20), channel_id=1, source_target_pairs={{1,0},{2,1},{3,2},{4,3},{5,4},{6,5},{7,6},{0,7},{9,8},{10,9},{11,1... | collective-permute-start | bytes 122888 | tf_op jit(solution)/shard_map/ppermute | solution.py:21
  34.4 198.8 %all-to-all-start = ((s32[32,1,64]{2,1,0:T(1,128)}), s32[32,1,64]{2,1,0:T(1,128)}, u32[]{:S(2)}, u32[]{:S(2)}) async-start(s32[32,1,64]{2,1,0:T(1,128)} %sub.44), calls=%async_computation | async-start | bytes 32768 | tf_op jit(solution)/shard_map/all_to_all | solution.py:109
  44.6 7.0 %copy-start.13 = (f32[17]{0:T(128)}, f32[17]{0:T(128)S(1)}, u32[]{:S(2)}) copy-start(f32[17]{0:T(128)S(1)} %and_select_fusion) | copy-start | bytes 208
  45.9 2.8 copy-start.2
  56.8 2.7 copy-start.5
  121.9 11.5 %copy-start.3 = (f32[1,128,16,128]{1,2,3,0:T(8,128)S(1)}, f32[1,128,16,128]{1,2,3,0:T(8,128)}, u32[]{:S(2)}) copy-start(f32[1,128,16,128]{1,2,3,0:T(8,128)} %copy.53) | copy-start | bytes 3145732
  121.9 11.5 %collective-permute-start.6 = (f32[5,128,16,1]{1,2,3,0:T(8,128)S(1)}, f32[5,128,16,1]{1,2,3,0:T(8,128)S(1)}, u32[]{:S(2)}, u32[]{:S(2)}) collective-permute-start(f32[5,128,16,1]{1,2,3,0:T(8,128)S(1)} %get-tuple-element.17), channel_id=1, source_target_pairs={{0,1},{1,2},{2,3},{3,4},{4,5},{5,6},{6,7},{7,0},{8,9},{9,10},{10,1... | collective-permute-start | bytes 122888 | tf_op jit(solution)/shard_map/ppermute | solution.py:18
  122.8 10.6 %collective-permute-start.7 = (f32[5,128,16,1]{1,2,3,0:T(8,128)S(1)}, f32[5,128,16,1]{1,2,3,0:T(8,128)S(1)}, u32[]{:S(2)}, u32[]{:S(2)}) collective-permute-start(f32[5,128,16,1]{1,2,3,0:T(8,128)S(1)} %get-tuple-element.18), channel_id=1, source_target_pairs={{1,0},{2,1},{3,2},{4,3},{5,4},{6,5},{7,6},{0,7},{9,8},{10,9},{11,1... | collective-permute-start | bytes 122888 | tf_op jit(solution)/shard_map/ppermute | solution.py:21
  126.2 10.4 %collective-permute-start.4 = (f32[5,128,1,128]{1,2,3,0:T(1,128)S(1)}, f32[5,128,1,128]{1,2,3,0:T(1,128)S(1)}, u32[]{:S(2)}, u32[]{:S(2)}) collective-permute-start(f32[5,128,1,128]{1,2,3,0:T(1,128)S(1)} %get-tuple-element.15), channel_id=1, source_target_pairs={{0,8},{8,16},{16,24},{1,9},{9,17},{17,25},{2,10},{10,18},{18,26},{... | collective-permute-start | bytes 983048 | tf_op jit(solution)/shard_map/ppermute | solution.py:18
  132.1 12.6 %collective-permute-start.5 = (f32[5,128,1,128]{1,2,3,0:T(1,128)S(1)}, f32[5,128,1,128]{1,2,3,0:T(1,128)S(1)}, u32[]{:S(2)}, u32[]{:S(2)}) collective-permute-start(f32[5,128,1,128]{1,2,3,0:T(1,128)S(1)} %get-tuple-element.16), channel_id=1, source_target_pairs={{8,0},{16,8},{24,16},{9,1},{17,9},{25,17},{10,2},{18,10},{26,18},{... | collective-permute-start | bytes 983048 | tf_op jit(solution)/shard_map/ppermute | solution.py:21
  134.8 10.1 %copy-start.14 = (f32[17]{0:T(128)S(1)}, f32[17]{0:T(128)}, u32[]{:S(2)}) copy-start(f32[17]{0:T(128)} %copy-done.13) | copy-start | bytes 208
  148.8 2.7 copy-start.4
  153.9 11.8 %copy-start.10 = (f32[2048]{0:T(1024)S(1)}, f32[2048]{0:T(1024)}, u32[]{:S(2)}) copy-start(f32[2048]{0:T(1024)} %convert_element_type.60) | copy-start | bytes 24580
  153.9 11.8 %copy-start.15 = (pred[2048]{0:T(1024)(128)(4,1)S(1)}, pred[2048]{0:T(1024)(128)(4,1)}, u32[]{:S(2)}) copy-start(pred[2048]{0:T(1024)(128)(4,1)} %get-tuple-element.7) | copy-start | bytes 6148
  153.9 11.8 %copy-start.16 = (f32[1024]{0:T(1024)S(1)}, f32[1024]{0:T(1024)}, u32[]{:S(2)}) copy-start(f32[1024]{0:T(1024)} %param.19) | copy-start | bytes 12292
  165.7 11.1 %copy-start.17 = (f32[1024]{0:T(1024)S(1)}, f32[1024]{0:T(1024)}, u32[]{:S(2)}) copy-start(f32[1024]{0:T(1024)} %param.21) | copy-start | bytes 12292
  176.8 8.1 %copy-start.9 = (pred[2048]{0:T(1024)(128)(4,1)S(1)}, pred[2048]{0:T(1024)(128)(4,1)}, u32[]{:S(2)}) copy-start(pred[2048]{0:T(1024)(128)(4,1)} %copy-done.8) | copy-start | bytes 6148
  214.9 2.7 copy-start.12
  233.2 56.9 %all-to-all-start.1 = ((bf16[32,64,512]{2,1,0:T(8,128)(2,1)}), bf16[32,64,512]{2,1,0:T(8,128)(2,1)}, u32[]{:S(2)}, u32[]{:S(2)}) async-start(bf16[32,64,512]{2,1,0:T(8,128)(2,1)} %reshape.146), calls=%async_computation.1 | async-start | bytes 4194304 | tf_op jit(solution)/shard_map/all_to_all | solution.py:108
  295.1 3.9 %copy-start.18 = (f32[1024]{0:T(1024)S(1)}, f32[1024]{0:T(1024)}, u32[]{:S(2)}) copy-start(f32[1024]{0:T(1024)} %param.26) | copy-start | bytes 12292
  (5 other events, 8.1 us)
where the time goes:
time: 310 us; the launch traced here: 304 us
  local copies, waits for them, and re-layouts  85.3 us (28%)
  other arithmetic  75.9 us (24%)
  matrix products  55.8 us (18%)
  waiting for transfers between devices  52.1 us (17%)
  starting transfers between devices  33.8 us (11%)
    all_to_all x1, waiting for transfers between devices, chemistry(): lax.all_to_all(packed, ('gx', 'gy'), split_axis=0, concat_axis=0, tiled=T...  42.2 us
    scatter-add x2, other arithmetic, radiate(): tendency = jnp.zeros_like(flat_fields).at[:, safe_index].add(jnp.where(li...  33.9 us
    unnamed x44, local copies, waits for them, and re-layouts  25.4 us
    gather x2, local copies, waits for them, and re-layouts, radiate(): jnp.take(flat_fields, safe_index, axis=1) * lit_mask[None, :]  24.2 us
    dot_general x2, matrix products, radiation_net(): lax.dot_general(rad_w2, layer_one, contract, preferred_element_type=jnp.f...  22.2 us
    dot_general x2, matrix products, radiation_net(): lax.dot_general(rad_w3, layer_two, contract, preferred_element_type=jnp.f...  16.1 us
    ppermute x4, starting transfers between devices, padded(): lax.ppermute(lax.slice_in_dim(block, block.shape[dim] - width, None, axis...  12.3 us
    add x2, other arithmetic, radiate(): return fields + tendency.reshape(fields.shape)  11.9 us
  transfers between devices with their start and end apart: 10, of which 3 were waited for; matrix products, arithmetic and copies ran while one was open for 61% of the time, Pallas kernels for 0%

commit v1 on v0

v1 whole, which is shorter than its diff:
```python
import functools

import jax
import jax.numpy as jnp
from jax import lax
from jax.experimental import pallas as pl
from jax.experimental.pallas import tpu as pltpu
from jax.sharding import PartitionSpec as P

BLOCK = 128
SEG = 2
STEPS = 2
GROUP = 2
VMEM = pl.BlockSpec(memory_space=pltpu.VMEM)
SMEM = pl.BlockSpec(memory_space=pltpu.SMEM)


def silu(x):
    half = 0.5 * x
    return half + half * jnp.tanh(half)


def lanes_of(shape):
    return lax.broadcasted_iota(jnp.int32, shape, len(shape) - 1)


def prep_kernel(rows, f_ref, c_ref, v_ref, lat_ref, lon_ref, edge_ref, cedge_ref):
    total = f_ref.shape[0] // rows
    levels = lat_ref.shape[1]
    width = f_ref.shape[1]
    edge_ref[...] = jnp.zeros_like(edge_ref)
    cedge_ref[...] = jnp.zeros_like(cedge_ref)

    def edges(ref, value, r):
        lane = lanes_of(value.shape)
        ref[...] = jnp.where(
            lane == r,
            pltpu.roll(value, r, axis=1),
            jnp.where(lane == rows + r, pltpu.roll(value, rows + 1 + r, axis=1), ref[...]),
        )

    def body(r, carry):
        value = f_ref[pl.ds(r, total, stride=rows), :]
        v_ref[r] = value
        edges(edge_ref, value, r)
        lat_ref[r] = c_ref[pl.ds(r, levels, stride=rows), :]
        lon = c_ref[pl.ds(levels * rows + r, levels, stride=rows), :]
        lon_ref[r] = lon
        edges(cedge_ref, lon, r)
        return carry

    lax.fori_loop(0, rows, body, 0)


def prep(fields, courant):
    count, levels, rows, cols = fields.shape
    total = count * levels
    f32 = jnp.float32
    return pl.pallas_call(
        functools.partial(prep_kernel, rows),
        out_shape=(
            jax.ShapeDtypeStruct((rows, total, cols), f32),
            jax.ShapeDtypeStruct((rows, levels, cols), f32),
            jax.ShapeDtypeStruct((rows, levels, cols), f32),
            jax.ShapeDtypeStruct((total, cols), f32),
            jax.ShapeDtypeStruct((levels, cols), f32),
        ),
        in_specs=[VMEM, VMEM],
        out_specs=(VMEM,) * 5,
        name="prep",
    )(fields.reshape(total * rows, cols), courant.reshape(2 * levels * rows, cols))


def step_kernel(
    last,
    flag_ref,
    v_ref,
    lat_ref,
    lon_ref,
    north_ref,
    south_ref,
    west_ref,
    east_ref,
    cnorth_ref,
    csouth_ref,
    cwest_ref,
    ceast_ref,
    lit_ref,
    w1_ref,
    b1_ref,
    w2_ref,
    b2_ref,
    w3_ref,
    *refs,
):
    rows, total, width = v_ref.shape
    levels = lat_ref.shape[1]
    count = total // levels
    if last:
        out_ref, src_ref, adv_ref, x_ref, one_ref, two_ref = refs
    else:
        out_ref, edge_ref, adv_ref, x_ref, one_ref, two_ref = refs
        edge_ref[...] = jnp.zeros_like(edge_ref)
    hidden = w1_ref.shape[0]
    lane = lanes_of((levels, width))

    def advect_row(r, slot):
        is_top = r == 0
        is_low = r == rows - 1
        up = jnp.maximum(r - 1, 0)
        down = jnp.minimum(r + 1, rows - 1)
        here = lat_ref[r]
        above = jnp.where(is_top, cnorth_ref[...], lat_ref[up])
        below = jnp.where(is_low, csouth_ref[...], lat_ref[down])
        face0 = 0.5 * (above + here) * jnp.where(is_top, flag_ref[0], 1.0)
        face1 = 0.5 * (here + below) * jnp.where(is_low, flag_ref[1], 1.0)
        pos0, neg0 = jnp.maximum(face0, 0.0), jnp.minimum(face0, 0.0)
        pos1, neg1 = jnp.maximum(face1, 0.0), jnp.minimum(face1, 0.0)

        def west_of(value, halo):
            return jnp.where(
                lane == 0, pltpu.roll(halo, width - rows - r, axis=1), pltpu.roll(value, 1, axis=1)
            )

        def east_of(value, halo):
            return jnp.where(
                lane == width - 1,
                pltpu.roll(halo, width - 1 - r, axis=1),
                pltpu.roll(value, width - 1, axis=1),
            )

        c = lon_ref[r]
        g0 = 0.5 * (west_of(c, cwest_ref[...]) + c)
        g1 = 0.5 * (c + east_of(c, ceast_ref[...]))
        gpos0, gneg0 = jnp.maximum(g0, 0.0), jnp.minimum(g0, 0.0)
        gpos1, gneg1 = jnp.maximum(g1, 0.0), jnp.minimum(g1, 0.0)
        for f in range(count):
            part = slice(f * levels, (f + 1) * levels)
            v = v_ref[r, part, :]
            vn = jnp.where(is_top, north_ref[part, :], v_ref[up, part, :])
            vs = jnp.where(is_low, south_ref[part, :], v_ref[down, part, :])
            vw = west_of(v, west_ref[part, :])
            ve = east_of(v, east_ref[part, :])
            f0 = pos0 * vn + neg0 * v
            f1 = pos1 * v + neg1 * vs
            h0 = gpos0 * vw + gneg0 * v
            h1 = gpos1 * v + gneg1 * ve
            new = v - (f1 - f0) - (h1 - h0)
            adv_ref[part, slot * width : (slot + 1) * width] = new
            x_ref[part, slot * width : (slot + 1) * width] = new.astype(jnp.bfloat16)

    def body(i, carry):
        for k in range(GROUP):
            advect_row(i * GROUP + k, k)
        chunk = 256
        for h in range(0, hidden, chunk):
            acc = jnp.dot(w1_ref[h : h + chunk, :], x_ref[...], preferred_element_type=jnp.float32)
            bias = jnp.concatenate([b1_ref[h : h + chunk, :]] * GROUP, axis=1)
            one_ref[h : h + chunk, :] = silu(acc + bias).astype(jnp.bfloat16)
        for h in range(0, hidden, chunk):
            acc = jnp.dot(w2_ref[h : h + chunk, :], one_ref[...], preferred_element_type=jnp.float32)
            bias = jnp.concatenate([b2_ref[h : h + chunk, :]] * GROUP, axis=1)
            two_ref[h : h + chunk, :] = silu(acc + bias).astype(jnp.bfloat16)
        lit = jnp.concatenate([lit_ref[i * GROUP + k] for k in range(GROUP)], axis=1)
        for h in range(0, total, chunk):
            heat = jnp.dot(w3_ref[h : h + chunk, :], two_ref[...], preferred_element_type=jnp.float32)
            new = adv_ref[h : h + chunk, :] + jnp.where(lit > 0.0, heat, 0.0)
            for k in range(GROUP):
                r = i * GROUP + k
                piece = new[:, k * width : (k + 1) * width]
                if last:
                    out_ref[pl.ds(h * rows + r, chunk, stride=rows), :] = piece
                    if h >= 2 * levels:
                        src_ref[
                            h - 2 * levels : h - 2 * levels + chunk,
                            pl.ds(pl.multiple_of(r * width, width), width),
                        ] = piece.astype(jnp.bfloat16)
                else:
                    out_ref[r, h : h + chunk, :] = piece
                    at = lanes_of(piece.shape)
                    edge_ref[h : h + chunk, :] = jnp.where(
                        at == r,
                        pltpu.roll(piece, r, axis=1),
                        jnp.where(
                            at == rows + r,
                            pltpu.roll(piece, rows + 1 + r, axis=1),
                            edge_ref[h : h + chunk, :],
                        ),
                    )
        return carry

    lax.fori_loop(0, rows // GROUP, body, 0)


def step(last, flags, v, lat, lon, halos, chalos, lit, nets):
    rows, total, cols = v.shape
    levels = lat.shape[1]
    hidden = nets[0].shape[0]
    f32, bf16 = jnp.float32, jnp.bfloat16
    if last:
        outs = (
            jax.ShapeDtypeStruct((total * rows, cols), f32),
            jax.ShapeDtypeStruct((2 * levels, rows * cols), bf16),
        )
    else:
        outs = (
            jax.ShapeDtypeStruct((rows, total, cols), f32),
            jax.ShapeDtypeStruct((total, cols), f32),
        )
    wide = GROUP * cols
    return pl.pallas_call(
        functools.partial(step_kernel, last),
        out_shape=outs,
        in_specs=[SMEM] + [VMEM] * 17,
        out_specs=(VMEM,) * 2,
        scratch_shapes=[
            pltpu.VMEM((total, wide), f32),
            pltpu.VMEM((total, wide), bf16),
            pltpu.VMEM((hidden, wide), bf16),
            pltpu.VMEM((hidden, wide), bf16),
        ],
        name="step_last" if last else "step_first",
    )(flags, v, lat, lon, *halos, *chalos, lit, *nets)


def pack_kernel(source_ref, target_ref, out_ref):
    tile = out_ref.shape[0]
    feats, cols = source_ref.shape
    slot = lax.broadcasted_iota(jnp.int32, (tile, cols), 0) + pl.program_id(0) * tile
    lane = lanes_of((tile, cols))
    match = slot == target_ref[...]
    for c in range(SEG):
        hit = (match & (lane % SEG == c)).astype(jnp.float32).astype(jnp.bfloat16)
        out_ref[:, c * feats : (c + 1) * feats] = lax.dot_general(
            hit, source_ref[...], (((1,), (1,)), ((), ())), preferred_element_type=jnp.float32
        ).astype(jnp.bfloat16)


def pack(source, target, slots):
    feats, cols = source.shape
    tile = 256
    return pl.pallas_call(
        pack_kernel,
        grid=(slots // tile,),
        out_shape=jax.ShapeDtypeStruct((slots, SEG * feats), jnp.bfloat16),
        in_specs=[
            pl.BlockSpec((feats, cols), lambda i: (0, 0)),
            pl.BlockSpec((1, cols), lambda i: (0, 0)),
        ],
        out_specs=pl.BlockSpec((tile, SEG * feats), lambda i: (i, 0)),
        name="pack",
    )(source, target)


def chem_kernel(arrived_ref, tag_ref, regrid_ref, w1_ref, b1_ref, w2_ref, out_ref, cell_ref):
    slots = arrived_ref.shape[0]
    feats = arrived_ref.shape[1] // SEG
    cells = out_ref.shape[0]
    segs = cells // SEG
    f32, bf16 = jnp.float32, jnp.bfloat16
    seg = lax.broadcasted_iota(jnp.int32, (segs, slots), 0) + pl.program_id(0) * segs
    pick = (seg == tag_ref[...]).astype(f32).astype(bf16)
    placed = jnp.dot(pick, arrived_ref[...], preferred_element_type=f32).astype(bf16)
    half = BLOCK // SEG
    row = lax.broadcasted_iota(jnp.int32, (BLOCK, BLOCK), 0)
    col = lax.broadcasted_iota(jnp.int32, (BLOCK, BLOCK), 1)
    order = (row == (col % half) * SEG + col // half).astype(f32).astype(bf16)
    for j in range(cells // BLOCK):
        mix = jnp.dot(regrid_ref[j], order, preferred_element_type=f32).astype(bf16)
        block = placed[j * half : (j + 1) * half, :]
        stacked = jnp.concatenate(
            [block[:, c * feats : (c + 1) * feats] for c in range(SEG)], axis=0
        )
        cell_ref[j * BLOCK : (j + 1) * BLOCK, :] = jnp.dot(
            mix, stacked, preferred_element_type=f32
        ).astype(bf16)
    hid = jnp.dot(cell_ref[...], w1_ref[...], preferred_element_type=f32) + b1_ref[...]
    out_ref[...] = jnp.dot(
        silu(hid).astype(bf16), w2_ref[...], preferred_element_type=f32
    ).astype(bf16)


def chem(arrived, tags, regrid, w1, b1, w2):
    slots, wide = arrived.shape
    feats = wide // SEG
    blocks = regrid.shape[0]
    per = 4
    hidden = w1.shape[1]
    whole = lambda *shape: pl.BlockSpec(shape, lambda i: (0,) * len(shape))
    return pl.pallas_call(
        chem_kernel,
        grid=(blocks // per,),
        out_shape=jax.ShapeDtypeStruct((blocks * BLOCK, feats), jnp.bfloat16),
        in_specs=[
            whole(slots, wide),
            whole(1, slots),
            pl.BlockSpec((per, BLOCK, BLOCK), lambda i: (i, 0, 0)),
            whole(feats, hidden),
            whole(1, hidden),
            whole(hidden, feats),
        ],
        out_specs=pl.BlockSpec((per * BLOCK, feats), lambda i: (i, 0)),
        scratch_shapes=[pltpu.VMEM((per * BLOCK, feats), jnp.bfloat16)],
        name="chem",
    )(arrived, tags, regrid, w1, b1, w2)


def shifted(axis, first, last, periodic):
    count = lax.axis_size(axis)
    forward = [(i, i + 1) for i in range(count - 1)]
    if periodic:
        forward.append((count - 1, 0))
    backward = [(target, source) for source, target in forward]
    return lax.ppermute(last, axis, forward), lax.ppermute(first, axis, backward)


def local(
    fields,
    courant,
    sun_columns,
    rad_w1,
    rad_b1,
    rad_w2,
    rad_b2,
    rad_w3,
    segment_route,
    regrid_weights,
    chem_w1,
    chem_b1,
    chem_w2,
):
    field_count, levels, rows, cols = fields.shape
    columns = rows * cols
    v, lat, lon, edge, cedge = prep(fields, courant)
    cwest, ceast = shifted("gy", cedge, cedge, True)
    cnorth, csouth = shifted("gx", lat[0], lat[rows - 1], False)

    place = lax.axis_index("gx")
    flags = jnp.stack([place > 0, place < lax.axis_size("gx") - 1]).astype(jnp.float32)
    slot_list = sun_columns.reshape(-1)
    lit = jnp.any(slot_list[:, None] == jnp.arange(columns)[None, :], axis=0)
    lit = lit.astype(jnp.float32).reshape(rows, 1, cols)

    def wide(bias):
        return jnp.broadcast_to(bias[:, None], (bias.shape[0], cols))

    nets = (rad_w1.T, wide(rad_b1), rad_w2.T, wide(rad_b2), rad_w3.T)

    segment_count = columns // SEG
    tile_count = lax.axis_size("gx") * lax.axis_size("gy")
    capacity = max(2, 2 * segment_count // tile_count)
    slots = tile_count * capacity
    destination = segment_route[0].reshape(-1)
    arrival_slot = segment_route[1].reshape(-1)
    segment_index = jnp.arange(segment_count)
    same_target = (destination[None, :] == destination[:, None]) & (
        segment_index[None, :] < segment_index[:, None]
    )
    order_rank = jnp.sum(same_target.astype(jnp.int32), axis=1)
    target_row = destination * capacity + order_rank
    placement = target_row[None, :] == jnp.arange(slots)[:, None]
    slot_tags = jnp.sum(jnp.where(placement, arrival_slot[None, :] + 1, 0), axis=1) - 1
    tags = lax.all_to_all(
        slot_tags.reshape(tile_count, capacity), ("gx", "gy"), split_axis=0, concat_axis=0, tiled=True
    ).reshape(1, slots)
    column_target = jnp.repeat(target_row, SEG).reshape(1, columns)

    for repeat in range(STEPS):
        last = repeat == STEPS - 1
        north, south = shifted("gx", v[0], v[rows - 1], False)
        west, east = shifted("gy", edge, edge, True)
        halos = (north, south, west, east)
        v, edge = step(last, flags, v, lat, lon, halos, (cnorth, csouth, cwest, ceast), lit, nets)
    source = edge
    packed = pack(source, column_target, slots).reshape(tile_count, capacity, SEG * 2 * levels)
    arrived = lax.all_to_all(packed, ("gx", "gy"), split_axis=0, concat_axis=0, tiled=True)
    arrived = arrived.reshape(slots, SEG * 2 * levels)
    output = chem(arrived, tags, regrid_weights[0, 0], chem_w1, chem_b1.reshape(1, -1), chem_w2)
    return (
        v.reshape(field_count, levels, rows, cols),
        output.reshape(1, 1, columns, 2 * levels),
    )


def solution(mesh):
    return jax.shard_map(
        local,
        mesh=mesh,
        in_specs=(
            P(None, None, "gx", "gy"),
            P(None, None, "gx", "gy"),
            P("gx", "gy", None),
            P(),
            P(),
            P(),
            P(),
            P(),
            P(None, "gx", "gy", None),
            P("gx", "gy", None, None, None),
            P(),
            P(),
            P(),
        ),
        out_specs=(P(None, None, "gx", "gy"), P("gx", "gy", None, None)),
        check_vma=False,
    )
```

time: 310 us -> 198 us (0.64); the launches traced: 304 us -> 197 us
  Pallas kernels: 0 us -> 81.9 us
  other arithmetic: 75.9 us -> 6.2 us
  local copies, waits for them, and re-layouts: 85.3 us -> 17.9 us
  matrix products: 55.8 us -> 0 us
  starting transfers between devices: 33.8 us -> 39 us
    pallas_call x0 -> x5, Pallas kernels: none -> 81.9 us  [the longest x2 53.1 us: step(): pl.pallas_call(functools.partial(step_kernel, last), out_shape=outs, in_s...]
    dot_general x8 -> x0, matrix products: 55.8 us -> none  [the longest x2 22.2 us: radiation_net(): lax.dot_general(rad_w2, layer_one, contract, preferred_element_type=jnp.f...]
    scatter-add x2 -> x0, other arithmetic: 33.9 us -> none  [radiate(): tendency = jnp.zeros_like(flat_fields).at[:, safe_index].add(jnp.where(li...]
    gather x2 -> x0, local copies, waits for them, and re-layouts: 24.2 us -> none  [radiate(): jnp.take(flat_fields, safe_index, axis=1) * lit_mask[None, :]]
    add x8 -> x2, other arithmetic: 20.6 us -> 0.01 us  [the longest x1 0.01 us: local(): arrival_slot[None, :] + 1]
    reshape x5 -> x1, local copies, waits for them, and re-layouts: 18 us -> 0.67 us  [local(): tags = lax.all_to_all(slot_tags.reshape(tile_count, capacity), ('gx', 'gy...]
    unnamed x44 -> x35, local copies, waits for them, and re-layouts: 25.4 us -> 9.14 us
    ppermute x8 -> x12, starting transfers between devices: 21.2 us -> 29.4 us  [the longest x6 15.1 us: shifted(): lax.ppermute(first, axis, backward)]
  transfers between devices with their start and end apart: 10 -> 14, of which waited for: 3 -> 3; matrix products, arithmetic and copies ran while one was open for 61% -> 10% of each run, Pallas kernels for 0% -> 17%
where the time goes in v1:
time: 198 us; the launch traced here: 197 us
  Pallas kernels  81.9 us (41%)
  waiting for transfers between devices  51.5 us (26%)
  starting transfers between devices  39 us (20%)
  local copies, waits for them, and re-layouts  17.9 us (9%)
  other arithmetic  6.2 us (3%)
    pallas_call x2, Pallas kernels, step(): pl.pallas_call(functools.partial(step_kernel, last), out_shape=outs, in_s...  53.1 us
    all_to_all x1, waiting for transfers between devices, local(): lax.all_to_all(packed, ('gx', 'gy'), split_axis=0, concat_axis=0, tiled=T...  48.1 us
    ppermute x6, starting transfers between devices, shifted(): lax.ppermute(first, axis, backward)  15.1 us
    ppermute x6, starting transfers between devices, shifted(): lax.ppermute(last, axis, forward)  14.2 us
    pallas_call x1, Pallas kernels, prep(): pl.pallas_call(functools.partial(prep_kernel, rows), out_shape=(jax.Shape...  11.2 us
    pallas_call x1, Pallas kernels, chem(): pl.pallas_call(chem_kernel, grid=(blocks // per,), out_shape=jax.ShapeDty...  9.65 us
    unnamed x35, local copies, waits for them, and re-layouts  9.14 us
    pallas_call x1, Pallas kernels, pack(): pl.pallas_call(pack_kernel, grid=(slots // tile,), out_shape=jax.ShapeDty...  7.96 us
  transfers between devices with their start and end apart: 14, of which 3 were waited for; matrix products, arithmetic and copies ran while one was open for 10% of the time, Pallas kernels for 17%

profile of v1, /device:TPU:0, one launch (start us, length us, event | category | flops | bytes accessed | tf_op | source)
XLA Modules:
  0.0 197.4 jit_solution(9110759458211668814)
XLA Ops:
  0.7 11.2 %prep.1 = (f32[16,512,128]{2,1,0:T(8,128)}, f32[16,128,128]{2,1,0:T(8,128)}, f32[16,128,128]{2,1,0:T(8,128)}, f32[512,128]{1,0:T(8,128)}, f32[128,128]{1,0:T(8,128)}) custom-call(f32[8192,128]{1,0:T(8,128)} %bitcast.37, f32[4096,128]{1,0:T(8,128)} %bitcast.38), custom_call_target="tpu_custom_call" | custom-call | tf_op jit(solution)/shard_map/prep/pallas_call | solution.py:59
  12.3 4.1 %collective-permute-start.3 = (f32[512,128]{1,0:T(8,128)}, f32[512,128]{1,0:T(8,128)}, u32[]{:S(2)}, u32[]{:S(2)}) collective-permute-start(f32[512,128]{1,0:T(8,128)} %get-tuple-element.14), channel_id=1, source_target_pairs={{1,0},{2,1},{3,2},{4,3},{5,4},{6,5},{7,6},{0,7},{9,8},{10,9},{11,1... | collective-permute-start | bytes 786440 | tf_op jit(solution)/shard_map/ppermute | solution.py:314
  17.3 3.9 %collective-permute-start.4 = (f32[128,128]{1,0:T(8,128)S(1)}, f32[128,128]{1,0:T(8,128)S(1)}, u32[]{:S(2)}, u32[]{:S(2)}) collective-permute-start(f32[128,128]{1,0:T(8,128)S(1)} %get-tuple-element.25), channel_id=1, source_target_pairs={{0,8},{8,16},{16,24},{1,9},{9,17},{17,25},{2,10},{10,18},{18,26},{... | collective-permute-start | bytes 196616 | tf_op jit(solution)/shard_map/ppermute | solution.py:314
  21.1 1.3 collective-permute-start.5
  22.4 1.8 slice_bitcast_fusion.2
  24.3 5.3 %collective-permute-start = (f32[512,128]{1,0:T(8,128)}, f32[512,128]{1,0:T(8,128)}, u32[]{:S(2)}, u32[]{:S(2)}) collective-permute-start(f32[512,128]{1,0:T(8,128)} %get-tuple-element.23), channel_id=1, source_target_pairs={{0,8},{8,16},{16,24},{1,9},{9,17},{17,25},{2,10},{10,18},{18,26},{... | collective-permute-start | bytes 786440 | tf_op jit(solution)/shard_map/ppermute | solution.py:314
  29.5 2.8 %fusion = pred[2048]{0:T(1024)(128)(4,1)S(1)} fusion(s32[2048]{0:T(1024)S(1)} %bitcast.48), kind=kLoop, calls=%fused_computation.1 | loop fusion | flops 8386560 | bytes 10240 | tf_op jit(solution)/shard_map/reduce_or | solution.py:341
  32.9 1.3 collective-permute-start.1
  34.4 2.6 %copy.25 = bf16[1024,1024]{0,1:T(8,128)(2,1)} copy(bf16[1024,1024]{1,0:T(8,128)(2,1)S(1)} %copy-done.1) | data formatting | bytes 4194304 | tf_op args[5]
  36.9 1.4 copy.24
  38.3 2.3 %copy.26 = bf16[1024,512]{0,1:T(8,128)(2,1)} copy(bf16[1024,512]{1,0:T(8,128)(2,1)} %param.20) | data formatting | bytes 2097152 | tf_op args[7]
  41.2 3.5 %collective-permute-start.7 = (f32[128,128]{1,0:T(8,128)S(1)}, f32[128,128]{1,0:T(8,128)S(1)}, u32[]{:S(2)}, u32[]{:S(2)}) collective-permute-start(f32[128,128]{1,0:T(8,128)S(1)} %copy-done.14), channel_id=1, source_target_pairs={{1,0},{2,1},{3,2},{4,3},{5,4},{6,5},{7,6},{0,7},{9,8},{10,9},{11,1... | collective-permute-start | bytes 196616 | tf_op jit(solution)/shard_map/ppermute | solution.py:314
  48.7 26.7 %step_first.1 = (f32[16,512,128]{2,1,0:T(8,128)}, f32[512,128]{1,0:T(8,128)}) custom-call(f32[2]{0:T(128)} %add_convert_fusion.flag_ref, f32[16,512,128]{2,1,0:T(8,128)} %get-tuple-element.11.v_ref, f32[16,128,128]{2,1,0:T(8,128)} %get-tuple-element.12.lat_ref, f32[16,128,128]{2,1,0:T(8,128)} %get-tuple-element.13.lon_ref, ...), custom_call_target="tpu_custom_call" | custom-call | tf_op jit(solution)/shard_map/step_first/pallas_call | solution.py:211
  75.5 3.6 %collective-permute-start.11 = (f32[512,128]{1,0:T(8,128)}, f32[512,128]{1,0:T(8,128)S(1)}, u32[]{:S(2)}, u32[]{:S(2)}) collective-permute-start(f32[512,128]{1,0:T(8,128)} %get-tuple-element.17), channel_id=1, source_target_pairs={{1,0},{2,1},{3,2},{4,3},{5,4},{6,5},{7,6},{0,7},{9,8},{10,9},{11,1... | collective-permute-start | bytes 786440 | tf_op jit(solution)/shard_map/ppermute | solution.py:314
  80.2 4.6 %collective-permute-start.8 = (f32[512,128]{1,0:T(8,128)S(1)}, f32[512,128]{1,0:T(8,128)S(1)}, u32[]{:S(2)}, u32[]{:S(2)}) collective-permute-start(f32[512,128]{1,0:T(8,128)S(1)} %get-tuple-element.21), channel_id=1, source_target_pairs={{0,8},{8,16},{16,24},{1,9},{9,17},{17,25},{2,10},{10,18},{18,26},{... | collective-permute-start | bytes 786440 | tf_op jit(solution)/shard_map/ppermute | solution.py:314
  84.8 1.3 collective-permute-start.9
  87.7 5.2 %all-to-all-start.1 = ((s32[32,1,64]{2,1,0:T(1,128)}), s32[32,1,64]{2,1,0:T(1,128)S(1)}, u32[]{:S(2)}, u32[]{:S(2)}) async-start(s32[32,1,64]{2,1,0:T(1,128)} %sub.7), calls=%async_computation.1 | async-start | bytes 32768 | tf_op jit(solution)/shard_map/all_to_all | solution.py:363
  94.0 2.1 %collective-permute-done.9.south_ref = f32[512,128]{1,0:T(8,128)S(1)} collective-permute-done((f32[512,128]{1,0:T(8,128)S(1)}, f32[512,128]{1,0:T(8,128)S(1)}, u32[]{:S(2)}, u32[]{:S(2)}) %collective-permute-start.9) | collective-permute-done | bytes 262176 | tf_op jit(solution)/shard_map/ppermute | solution.py:314
  97.6 26.4 %step_last.1 = (f32[8192,128]{1,0:T(8,128)}, bf16[256,2048]{1,0:T(8,128)(2,1)}) custom-call(f32[2]{0:T(128)} %add_convert_fusion.flag_ref, f32[16,512,128]{2,1,0:T(8,128)} %get-tuple-element.16.v_ref, f32[16,128,128]{2,1,0:T(8,128)} %get-tuple-element.12.lat_ref, f32[16,128,128]{2,1,0:T(8,128)} %get-tuple-element.13.lon_ref, f32[512,128]{1,0:T(8,128)} %copy-done.9, ...), custom_call_target="tpu_custom_call" | custom-call | tf_op jit(solution)/shard_map/step_last/pallas_call | solution.py:211
  124.0 8.0 %pack.1 = bf16[2048,512]{1,0:T(8,128)(2,1)} custom-call(bf16[256,2048]{1,0:T(8,128)(2,1)} %get-tuple-element.19.source_ref, s32[1,2048]{1,0:T(1,128)} %reshape_reshape.3.target_ref), custom_call_target="tpu_custom_call" | custom-call | tf_op jit(solution)/shard_map/pack/pallas_call | solution.py:242
  131.9 4.4 %all-to-all-start = ((bf16[32,64,512]{2,1,0:T(8,128)(2,1)}), bf16[32,64,512]{2,1,0:T(8,128)(2,1)S(1)}, u32[]{:S(2)}, u32[]{:S(2)}) async-start(bf16[32,64,512]{2,1,0:T(8,128)(2,1)} %bitcast.35), calls=%async_computation | async-start | bytes 4194304 | tf_op jit(solution)/shard_map/all_to_all | solution.py:376
  138.2 48.1 %all-to-all-done = bf16[32,64,512]{2,1,0:T(8,128)(2,1)S(1)} async-done(((bf16[32,64,512]{2,1,0:T(8,128)(2,1)}), bf16[32,64,512]{2,1,0:T(8,128)(2,1)S(1)}, u32[]{:S(2)}, u32[]{:S(2)}) %all-to-all-start) | async-done | bytes 2097184 | tf_op jit(solution)/shard_map/all_to_all | solution.py:376
  186.4 1.3 copy-done
  187.7 9.7 %chem.1 = bf16[2048,256]{1,0:T(8,128)(2,1)} custom-call(bf16[2048,512]{1,0:T(8,128)(2,1)} %bitcast.36, s32[1,2048]{1,0:T(1,128)} %reshape.85.tag_ref, bf16[16,128,128]{2,1,0:T(8,128)(2,1)} %bitcast.40, bf16[256,1024]{1,0:T(8,128)(2,1)} %w1_ref.1, f32[1,1024]{1,0:T(1,128)} %bitcast.46, bf16[1024,256]{1,0:T(8,128)(2,1)} %w2_ref.1), custom_call_target="tpu_custom_call" | custom-call | tf_op jit(solution)/shard_map/chem/pallas_call | solution.py:290
  (63 shorter events, 13.7 us)
Async XLA Ops:
  0.6 28.9 %copy-start.15 = (s32[1,1,2048]{2,1,0:T(1,128)S(1)}, s32[1,1,2048]{2,1,0:T(1,128)}, u32[]{:S(2)}) copy-start(s32[1,1,2048]{2,1,0:T(1,128)} %param.15) | copy-start | bytes 24580
  0.6 31.7 %copy-start.11 = (s32[2,1,1,1024]{3,2,1,0:T(1,128)S(1)}, s32[2,1,1,1024]{3,2,1,0:T(1,128)}, u32[]{:S(2)}) copy-start(s32[2,1,1,1024]{3,2,1,0:T(1,128)} %param.21) | copy-start | bytes 24580
  0.7 33.7 %copy-start.1 = (bf16[1024,1024]{1,0:T(8,128)(2,1)S(1)}, bf16[1024,1024]{1,0:T(8,128)(2,1)}, u32[]{:S(2)}) copy-start(bf16[1024,1024]{1,0:T(8,128)(2,1)} %param.18) | copy-start | bytes 6291460
  11.8 25.1 %copy-start.2 = (bf16[512,1024]{1,0:T(8,128)(2,1)S(1)}, bf16[512,1024]{1,0:T(8,128)(2,1)}, u32[]{:S(2)}) copy-start(bf16[512,1024]{1,0:T(8,128)(2,1)} %param.16) | copy-start | bytes 3145732
  11.8 34.9 %collective-permute-start.2 = (f32[512,128]{1,0:T(8,128)}, f32[512,128]{1,0:T(8,128)}, u32[]{:S(2)}, u32[]{:S(2)}) collective-permute-start(f32[512,128]{1,0:T(8,128)} %get-tuple-element.14), channel_id=1, source_target_pairs={{0,1},{1,2},{2,3},{3,4},{4,5},{5,6},{6,7},{7,0},{8,9},{9,10},{10,1... | collective-permute-start | bytes 786440 | tf_op jit(solution)/shard_map/ppermute | solution.py:314
  12.3 34.4 %collective-permute-start.3 = (f32[512,128]{1,0:T(8,128)}, f32[512,128]{1,0:T(8,128)}, u32[]{:S(2)}, u32[]{:S(2)}) collective-permute-start(f32[512,128]{1,0:T(8,128)} %get-tuple-element.14), channel_id=1, source_target_pairs={{1,0},{2,1},{3,2},{4,3},{5,4},{6,5},{7,6},{0,7},{9,8},{10,9},{11,1... | collective-permute-start | bytes 786440 | tf_op jit(solution)/shard_map/ppermute | solution.py:314
  17.3 15.6 %collective-permute-start.4 = (f32[128,128]{1,0:T(8,128)S(1)}, f32[128,128]{1,0:T(8,128)S(1)}, u32[]{:S(2)}, u32[]{:S(2)}) collective-permute-start(f32[128,128]{1,0:T(8,128)S(1)} %get-tuple-element.25), channel_id=1, source_target_pairs={{0,8},{8,16},{16,24},{1,9},{9,17},{17,25},{2,10},{10,18},{18,26},{... | collective-permute-start | bytes 196616 | tf_op jit(solution)/shard_map/ppermute | solution.py:314
  21.1 13.1 %collective-permute-start.5 = (f32[128,128]{1,0:T(8,128)S(1)}, f32[128,128]{1,0:T(8,128)S(1)}, u32[]{:S(2)}, u32[]{:S(2)}) collective-permute-start(f32[128,128]{1,0:T(8,128)S(1)} %get-tuple-element.24), channel_id=1, source_target_pairs={{8,0},{16,8},{24,16},{9,1},{17,9},{25,17},{10,2},{18,10},{26,18},{... | collective-permute-start | bytes 196616 | tf_op jit(solution)/shard_map/ppermute | solution.py:314
  24.3 22.4 %collective-permute-start = (f32[512,128]{1,0:T(8,128)}, f32[512,128]{1,0:T(8,128)}, u32[]{:S(2)}, u32[]{:S(2)}) collective-permute-start(f32[512,128]{1,0:T(8,128)} %get-tuple-element.23), channel_id=1, source_target_pairs={{0,8},{8,16},{16,24},{1,9},{9,17},{17,25},{2,10},{10,18},{18,26},{... | collective-permute-start | bytes 786440 | tf_op jit(solution)/shard_map/ppermute | solution.py:314
  32.9 7.7 %copy-start.3 = (f32[128,128]{1,0:T(8,128)}, f32[128,128]{1,0:T(8,128)S(1)}, u32[]{:S(2)}) copy-start(f32[128,128]{1,0:T(8,128)S(1)} %collective-permute-done.4.cnorth_ref) | copy-start | bytes 196612
  32.9 13.8 %collective-permute-start.1 = (f32[512,128]{1,0:T(8,128)}, f32[512,128]{1,0:T(8,128)}, u32[]{:S(2)}, u32[]{:S(2)}) collective-permute-start(f32[512,128]{1,0:T(8,128)} %get-tuple-element.22), channel_id=1, source_target_pairs={{8,0},{16,8},{24,16},{9,1},{17,9},{25,17},{10,2},{18,10},{26,18},{... | collective-permute-start | bytes 786440 | tf_op jit(solution)/shard_map/ppermute | solution.py:314
  34.2 6.4 %copy-start.4 = (f32[128,128]{1,0:T(8,128)}, f32[128,128]{1,0:T(8,128)S(1)}, u32[]{:S(2)}) copy-start(f32[128,128]{1,0:T(8,128)S(1)} %collective-permute-done.5.csouth_ref) | copy-start | bytes 196612
  34.2 7.0 %collective-permute-start.6 = (f32[128,128]{1,0:T(8,128)}, f32[128,128]{1,0:T(8,128)S(1)}, u32[]{:S(2)}, u32[]{:S(2)}) collective-permute-start(f32[128,128]{1,0:T(8,128)} %get-tuple-element.15), channel_id=1, source_target_pairs={{0,1},{1,2},{2,3},{3,4},{4,5},{5,6},{6,7},{7,0},{8,9},{9,10},{10,1... | collective-permute-start | bytes 196616 | tf_op jit(solution)/shard_map/ppermute | solution.py:314
  34.3 6.9 %copy-start.14 = (f32[128,128]{1,0:T(8,128)S(1)}, f32[128,128]{1,0:T(8,128)}, u32[]{:S(2)}) copy-start(f32[128,128]{1,0:T(8,128)} %get-tuple-element.15) | copy-start | bytes 196612
  34.3 12.4 %copy-start.12 = (f32[1024]{0:T(1024)S(1)}, f32[1024]{0:T(1024)}, u32[]{:S(2)}) copy-start(f32[1024]{0:T(1024)} %param.17) | copy-start | bytes 12292
  34.3 13.4 %copy-start.13 = (f32[1024]{0:T(1024)S(1)}, f32[1024]{0:T(1024)}, u32[]{:S(2)}) copy-start(f32[1024]{0:T(1024)} %param.19) | copy-start | bytes 12292
  41.2 7.5 %copy-start.5 = (f32[128,128]{1,0:T(8,128)}, f32[128,128]{1,0:T(8,128)S(1)}, u32[]{:S(2)}) copy-start(f32[128,128]{1,0:T(8,128)S(1)} %collective-permute-done.6.cwest_ref) | copy-start | bytes 196612
  41.2 5.4 %collective-permute-start.7 = (f32[128,128]{1,0:T(8,128)S(1)}, f32[128,128]{1,0:T(8,128)S(1)}, u32[]{:S(2)}, u32[]{:S(2)}) collective-permute-start(f32[128,128]{1,0:T(8,128)S(1)} %copy-done.14), channel_id=1, source_target_pairs={{1,0},{2,1},{3,2},{4,3},{5,4},{6,5},{7,6},{0,7},{9,8},{10,9},{11,1... | collective-permute-start | bytes 196616 | tf_op jit(solution)/shard_map/ppermute | solution.py:314
  75.5 20.6 %collective-permute-start.10 = (f32[512,128]{1,0:T(8,128)}, f32[512,128]{1,0:T(8,128)S(1)}, u32[]{:S(2)}, u32[]{:S(2)}) collective-permute-start(f32[512,128]{1,0:T(8,128)} %get-tuple-element.17), channel_id=1, source_target_pairs={{0,1},{1,2},{2,3},{3,4},{4,5},{5,6},{6,7},{7,0},{8,9},{9,10},{10,1... | collective-permute-start | bytes 786440 | tf_op jit(solution)/shard_map/ppermute | solution.py:314
  75.5 20.6 %collective-permute-start.11 = (f32[512,128]{1,0:T(8,128)}, f32[512,128]{1,0:T(8,128)S(1)}, u32[]{:S(2)}, u32[]{:S(2)}) collective-permute-start(f32[512,128]{1,0:T(8,128)} %get-tuple-element.17), channel_id=1, source_target_pairs={{1,0},{2,1},{3,2},{4,3},{5,4},{6,5},{7,6},{0,7},{9,8},{10,9},{11,1... | collective-permute-start | bytes 786440 | tf_op jit(solution)/shard_map/ppermute | solution.py:314
  80.2 13.8 %collective-permute-start.8 = (f32[512,128]{1,0:T(8,128)S(1)}, f32[512,128]{1,0:T(8,128)S(1)}, u32[]{:S(2)}, u32[]{:S(2)}) collective-permute-start(f32[512,128]{1,0:T(8,128)S(1)} %get-tuple-element.21), channel_id=1, source_target_pairs={{0,8},{8,16},{16,24},{1,9},{9,17},{17,25},{2,10},{10,18},{18,26},{... | collective-permute-start | bytes 786440 | tf_op jit(solution)/shard_map/ppermute | solution.py:314
  84.8 11.3 %collective-permute-start.9 = (f32[512,128]{1,0:T(8,128)S(1)}, f32[512,128]{1,0:T(8,128)S(1)}, u32[]{:S(2)}, u32[]{:S(2)}) collective-permute-start(f32[512,128]{1,0:T(8,128)S(1)} %get-tuple-element.20), channel_id=1, source_target_pairs={{8,0},{16,8},{24,16},{9,1},{17,9},{25,17},{10,2},{18,10},{26,18},{... | collective-permute-start | bytes 786440 | tf_op jit(solution)/shard_map/ppermute | solution.py:314
  87.7 44.2 %all-to-all-start.1 = ((s32[32,1,64]{2,1,0:T(1,128)}), s32[32,1,64]{2,1,0:T(1,128)S(1)}, u32[]{:S(2)}, u32[]{:S(2)}) async-start(s32[32,1,64]{2,1,0:T(1,128)} %sub.7), calls=%async_computation.1 | async-start | bytes 32768 | tf_op jit(solution)/shard_map/all_to_all | solution.py:363
  131.9 54.5 %all-to-all-start = ((bf16[32,64,512]{2,1,0:T(8,128)(2,1)}), bf16[32,64,512]{2,1,0:T(8,128)(2,1)S(1)}, u32[]{:S(2)}, u32[]{:S(2)}) async-start(bf16[32,64,512]{2,1,0:T(8,128)(2,1)} %bitcast.35), calls=%async_computation | async-start | bytes 4194304 | tf_op jit(solution)/shard_map/all_to_all | solution.py:376
  (6 other events, 7.7 us)

commit v2 on v1

--- a/solution.py
+++ b/solution.py
@@ -24,32 +24,36 @@
     return lax.broadcasted_iota(jnp.int32, shape, len(shape) - 1)
 
 
-def prep_kernel(rows, f_ref, c_ref, v_ref, lat_ref, lon_ref, edge_ref, cedge_ref):
+def prep_kernel(rows, f_ref, c_ref, v_ref, lat_ref, lon_ref, rim_ref, edge_ref):
     total = f_ref.shape[0] // rows
     levels = lat_ref.shape[1]
-    width = f_ref.shape[1]
     edge_ref[...] = jnp.zeros_like(edge_ref)
-    cedge_ref[...] = jnp.zeros_like(cedge_ref)
-
-    def edges(ref, value, r):
+
+    def edges(part, value, r):
         lane = lanes_of(value.shape)
-        ref[...] = jnp.where(
+        edge_ref[part, :] = jnp.where(
             lane == r,
             pltpu.roll(value, r, axis=1),
-            jnp.where(lane == rows + r, pltpu.roll(value, rows + 1 + r, axis=1), ref[...]),
+            jnp.where(
+                lane == rows + r, pltpu.roll(value, rows + 1 + r, axis=1), edge_ref[part, :]
+            ),
         )
 
     def body(r, carry):
         value = f_ref[pl.ds(r, total, stride=rows), :]
         v_ref[r] = value
-        edges(edge_ref, value, r)
+        edges(slice(0, total), value, r)
         lat_ref[r] = c_ref[pl.ds(r, levels, stride=rows), :]
         lon = c_ref[pl.ds(levels * rows + r, levels, stride=rows), :]
         lon_ref[r] = lon
-        edges(cedge_ref, lon, r)
+        edges(slice(total, total + levels), lon, r)
         return carry
 
     lax.fori_loop(0, rows, body, 0)
+    for k, r in enumerate((0, rows - 1)):
+        rim_ref[k, :total, :] = v_ref[r].astype(jnp.bfloat16)
+        rim_ref[k, total:, :] = lat_ref[r].astype(jnp.bfloat16)
+    rim_ref[2] = edge_ref[...].astype(jnp.bfloat16)
 
 
 def prep(fields, courant):
@@ -62,13 +66,124 @@
             jax.ShapeDtypeStruct((rows, total, cols), f32),
             jax.ShapeDtypeStruct((rows, levels, cols), f32),
             jax.ShapeDtypeStruct((rows, levels, cols), f32),
-            jax.ShapeDtypeStruct((total, cols), f32),
-            jax.ShapeDtypeStruct((levels, cols), f32),
+            jax.ShapeDtypeStruct((3, total + levels, cols), jnp.bfloat16),
         ),
         in_specs=[VMEM, VMEM],
-        out_specs=(VMEM,) * 5,
+        out_specs=(VMEM,) * 4,
+        scratch_shapes=[pltpu.VMEM((total + levels, cols), f32)],
         name="prep",
     )(fields.reshape(total * rows, cols), courant.reshape(2 * levels * rows, cols))
+
+
+def exchange_kernel(extra, nx, ny, rim_ref, *refs):
+    refs = list(refs)
+    ins, refs = refs[:extra], refs[extra:]
+    halo_ref, refs = refs[0], refs[1:]
+    outs, refs = refs[:extra], refs[extra:]
+    land_ref, send_sem, recv_sem = refs
+    gx, gy = lax.axis_index("gx"), lax.axis_index("gy")
+    west, east = lax.rem(gy + ny - 1, ny), lax.rem(gy + 1, ny)
+    barrier = pltpu.get_barrier_semaphore()
+    mesh_id = pl.DeviceIdType.MESH
+    has_north, has_south = gx > 0, gx < nx - 1
+
+    def greet(target):
+        pl.semaphore_signal(barrier, inc=1, device_id=target, device_id_type=mesh_id)
+
+    land_ref[0] = jnp.zeros_like(land_ref[0])
+    land_ref[1] = jnp.zeros_like(land_ref[1])
+    greet((gx, west))
+    greet((gx, east))
+
+    @pl.when(has_north)
+    def _():
+        greet((gx - 1, gy))
+
+    @pl.when(has_south)
+    def _():
+        greet((gx + 1, gy))
+
+    pl.semaphore_wait(barrier, 2 + jnp.minimum(gx, 1) + jnp.minimum(nx - 1 - gx, 1))
+
+    def copy(source, slot, target):
+        return pltpu.make_async_remote_copy(
+            src_ref=rim_ref.at[source],
+            dst_ref=land_ref.at[slot],
+            send_sem=send_sem.at[slot],
+            recv_sem=recv_sem.at[slot],
+            device_id=target,
+            device_id_type=mesh_id,
+        )
+
+    to_south = copy(1, 0, (jnp.minimum(gx + 1, nx - 1), gy))
+    to_north = copy(0, 1, (jnp.maximum(gx - 1, 0), gy))
+    to_east = copy(2, 2, (gx, east))
+    to_west = copy(2, 3, (gx, west))
+
+    @pl.when(has_south)
+    def _():
+        to_south.start()
+
+    @pl.when(has_north)
+    def _():
+        to_north.start()
+
+    to_east.start()
+    to_west.start()
+    if extra:
+        for k in range(3):
+            outs[k][...] = ins[k][...].T
+        for k in range(3, 5):
+            outs[k][...] = jnp.broadcast_to(ins[k][...], outs[k].shape)
+        slots, lit_ref = ins[5], outs[5]
+        shape = (slots.shape[0], lit_ref.shape[2])
+
+        def mark(r, carry):
+            hit = slots[...] == lanes_of(shape) + r * shape[1]
+            lit_ref[r] = jnp.max(jnp.where(hit, 1.0, 0.0), axis=0, keepdims=True)
+            return carry
+
+        lax.fori_loop(0, lit_ref.shape[0], mark, 0)
+
+    @pl.when(has_south)
+    def _():
+        to_south.wait_send()
+
+    @pl.when(has_north)
+    def _():
+        to_north.wait_send()
+
+    to_east.wait()
+    to_west.wait()
+
+    @pl.when(has_north)
+    def _():
+        to_south.wait_recv()
+
+    @pl.when(has_south)
+    def _():
+        to_north.wait_recv()
+
+    for k in range(4):
+        halo_ref[k] = land_ref[k].astype(jnp.float32)
+
+
+def exchange(rim, number, ins, shapes):
+    _, depth, cols = rim.shape
+    nx, ny = lax.axis_size("gx"), lax.axis_size("gy")
+    return pl.pallas_call(
+        functools.partial(exchange_kernel, len(ins), nx, ny),
+        out_shape=(jax.ShapeDtypeStruct((4, depth, cols), jnp.float32), *shapes),
+        in_specs=[VMEM] * (1 + len(ins)),
+        out_specs=(VMEM,) * (1 + len(shapes)),
+        scratch_shapes=[
+            pltpu.VMEM((4, depth, cols), jnp.bfloat16),
+            pltpu.SemaphoreType.DMA((4,)),
+            pltpu.SemaphoreType.DMA((4,)),
+        ],
+        compiler_params=pltpu.CompilerParams(collective_id=number, has_side_effects=True),
+        name="exchange%d" % number,
+    )(rim, *ins)
 
 
 def step_kernel(
@@ -77,14 +192,8 @@
     v_ref,
     lat_ref,
     lon_ref,
-    north_ref,
-    south_ref,
-    west_ref,
-    east_ref,
-    cnorth_ref,
-    csouth_ref,
-    cwest_ref,
-    ceast_ref,
+    halo_ref,
+    chalo_ref,
     lit_ref,
     w1_ref,
     b1_ref,
@@ -99,7 +208,7 @@
     if last:
         out_ref, src_ref, adv_ref, x_ref, one_ref, two_ref = refs
     else:
-        out_ref, edge_ref, adv_ref, x_ref, one_ref, two_ref = refs
+        out_ref, rim_ref, adv_ref, x_ref, one_ref, two_ref, edge_ref = refs
         edge_ref[...] = jnp.zeros_like(edge_ref)
     hidden = w1_ref.shape[0]
     lane = lanes_of((levels, width))
@@ -110,8 +219,8 @@
         up = jnp.maximum(r - 1, 0)
         down = jnp.minimum(r + 1, rows - 1)
         here = lat_ref[r]
-        above = jnp.where(is_top, cnorth_ref[...], lat_ref[up])
-        below = jnp.where(is_low, csouth_ref[...], lat_ref[down])
+        above = jnp.where(is_top, chalo_ref[0, chalo_ref.shape[1] - levels :, :], lat_ref[up])
+        below = jnp.where(is_low, chalo_ref[1, chalo_ref.shape[1] - levels :, :], lat_ref[down])
         face0 = 0.5 * (above + here) * jnp.where(is_top, flag_ref[0], 1.0)
         face1 = 0.5 * (here + below) * jnp.where(is_low, flag_ref[1], 1.0)
         pos0, neg0 = jnp.maximum(face0, 0.0), jnp.minimum(face0, 0.0)
@@ -130,17 +239,17 @@
             )
 
         c = lon_ref[r]
-        g0 = 0.5 * (west_of(c, cwest_ref[...]) + c)
-        g1 = 0.5 * (c + east_of(c, ceast_ref[...]))
+        g0 = 0.5 * (west_of(c, chalo_ref[2, chalo_ref.shape[1] - levels :, :]) + c)
+        g1 = 0.5 * (c + east_of(c, chalo_ref[3, chalo_ref.shape[1] - levels :, :]))
         gpos0, gneg0 = jnp.maximum(g0, 0.0), jnp.minimum(g0, 0.0)
         gpos1, gneg1 = jnp.maximum(g1, 0.0), jnp.minimum(g1, 0.0)
         for f in range(count):
             part = slice(f * levels, (f + 1) * levels)
             v = v_ref[r, part, :]
-            vn = jnp.where(is_top, north_ref[part, :], v_ref[up, part, :])
-            vs = jnp.where(is_low, south_ref[part, :], v_ref[down, part, :])
-            vw = west_of(v, west_ref[part, :])
-            ve = east_of(v, east_ref[part, :])
+            vn = jnp.where(is_top, halo_ref[0, part, :], v_ref[up, part, :])
+            vs = jnp.where(is_low, halo_ref[1, part, :], v_ref[down, part, :])
+            vw = west_of(v, halo_ref[2, part, :])
+            ve = east_of(v, halo_ref[3, part, :])
             f0 = pos0 * vn + neg0 * v
             f1 = pos1 * v + neg1 * vs
             h0 = gpos0 * vw + gneg0 * v
@@ -190,9 +299,13 @@
         return carry
 
     lax.fori_loop(0, rows // GROUP, body, 0)
-
-
-def step(last, flags, v, lat, lon, halos, chalos, lit, nets):
+    if not last:
+        rim_ref[0] = out_ref[0].astype(jnp.bfloat16)
+        rim_ref[1] = out_ref[rows - 1].astype(jnp.bfloat16)
+        rim_ref[2] = edge_ref[...].astype(jnp.bfloat16)
+
+
+def step(last, flags, v, lat, lon, halo, chalo, lit, nets):
     rows, total, cols = v.shape
     levels = lat.shape[1]
     hidden = nets[0].shape[0]
@@ -205,22 +318,23 @@
     else:
         outs = (
             jax.ShapeDtypeStruct((rows, total, cols), f32),
-            jax.ShapeDtypeStruct((total, cols), f32),
+            jax.ShapeDtypeStruct((3, total, cols), bf16),
         )
     wide = GROUP * cols
     return pl.pallas_call(
         functools.partial(step_kernel, last),
         out_shape=outs,
-        in_specs=[SMEM] + [VMEM] * 17,
+        in_specs=[SMEM] + [VMEM] * 11,
         out_specs=(VMEM,) * 2,
         scratch_shapes=[
             pltpu.VMEM((total, wide), f32),
             pltpu.VMEM((total, wide), bf16),
             pltpu.VMEM((hidden, wide), bf16),
             pltpu.VMEM((hidden, wide), bf16),
-        ],
+        ]
+        + ([] if last else [pltpu.VMEM((total, cols), f32)]),
         name="step_last" if last else "step_first",
-    )(flags, v, lat, lon, *halos, *chalos, lit, *nets)
+    )(flags, v, lat, lon, halo, chalo, lit, *nets)
 
 
 def pack_kernel(source_ref, target_ref, out_ref):
@@ -305,15 +419,6 @@
     )(arrived, tags, regrid, w1, b1, w2)
 
 
-def shifted(axis, first, last, periodic):
-    count = lax.axis_size(axis)
-    forward = [(i, i + 1) for i in range(count - 1)]
-    if periodic:
-        forward.append((count - 1, 0))
-    backward = [(target, source) for source, target in forward]
-    return lax.ppermute(last, axis, forward), lax.ppermute(first, axis, backward)
-
-
 def local(
     fields,
     courant,
@@ -331,20 +436,25 @@
 ):
     field_count, levels, rows, cols = fields.shape
     columns = rows * cols
-    v, lat, lon, edge, cedge = prep(fields, courant)
-    cwest, ceast = shifted("gy", cedge, cedge, True)
-    cnorth, csouth = shifted("gx", lat[0], lat[rows - 1], False)
-
+    v, lat, lon, rim = prep(fields, courant)
     place = lax.axis_index("gx")
     flags = jnp.stack([place > 0, place < lax.axis_size("gx") - 1]).astype(jnp.float32)
-    slot_list = sun_columns.reshape(-1)
-    lit = jnp.any(slot_list[:, None] == jnp.arange(columns)[None, :], axis=0)
-    lit = lit.astype(jnp.float32).reshape(rows, 1, cols)
-
-    def wide(bias):
-        return jnp.broadcast_to(bias[:, None], (bias.shape[0], cols))
-
-    nets = (rad_w1.T, wide(rad_b1), rad_w2.T, wide(rad_b2), rad_w3.T)
+    bf16, f32 = jnp.bfloat16, jnp.float32
+    ins = (
+        rad_w1,
+        rad_w2,
+        rad_w3,
+        rad_b1.reshape(-1, 1),
+        rad_b2.reshape(-1, 1),
+        sun_columns.reshape(-1, 1),
+    )
+    shapes = (
+        *(jax.ShapeDtypeStruct(w.shape[::-1], bf16) for w in ins[:3]),
+        *(jax.ShapeDtypeStruct((b.shape[0], cols), f32) for b in ins[3:5]),
+        jax.ShapeDtypeStruct((rows, 1, cols), f32),
+    )
+    chalo, w1, w2, w3, b1, b2, lit = exchange(rim, 0, ins, shapes)
+    nets = (w1, b1, w2, b2, w3)
 
     segment_count = columns // SEG
     tile_count = lax.axis_size("gx") * lax.axis_size("gy")
@@ -365,13 +475,13 @@
     ).reshape(1, slots)
     column_target = jnp.repeat(target_row, SEG).reshape(1, columns)
 
+    halo = chalo
     for repeat in range(STEPS):
         last = repeat == STEPS - 1
-        north, south = shifted("gx", v[0], v[rows - 1], False)
-        west, east = shifted("gy", edge, edge, True)
-        halos = (north, south, west, east)
-        v, edge = step(last, flags, v, lat, lon, halos, (cnorth, csouth, cwest, ceast), lit, nets)
-    source = edge
+        v, rim = step(last, flags, v, lat, lon, halo, chalo, lit, nets)
+        if not last:
+            (halo,) = exchange(rim, repeat + 1, (), ())
+    source = rim
     packed = pack(source, column_target, slots).reshape(tile_count, capacity, SEG * 2 * levels)
     arrived = lax.all_to_all(packed, ("gx", "gy"), split_axis=0, concat_axis=0, tiled=True)
     arrived = arrived.reshape(slots, SEG * 2 * levels)

time: 198 us -> 184 us (0.929)
  Pallas kernels: 81.9 us -> 111 us
  starting transfers between devices: 39 us -> 10.6 us
  local copies, waits for them, and re-layouts: 17.9 us -> 9.78 us
  waiting for transfers between devices: 51.5 us -> 48.1 us
  other arithmetic: 6.2 us -> 3.49 us
    ppermute x12 -> x0, starting transfers between devices: 29.4 us -> none  [the longest x6 15.1 us: shifted(): lax.ppermute(first, axis, backward)]
    pallas_call x0 -> x2, Pallas kernels: none -> 28.7 us  [exchange(): pl.pallas_call(functools.partial(exchange_kernel, len(ins), nx, ny), out_...]
    unnamed x35 -> x2, local copies, waits for them, and re-layouts: 9.14 us -> 1.34 us
    reshape x0 -> x3, local copies, waits for them, and re-layouts: none -> 5.46 us  [the longest x1 2.04 us: local(): sun_columns.reshape(-1, 1)]
    squeeze x3 -> x0, local copies, waits for them, and re-layouts: 3.79 us -> none  [the longest x2 2.91 us: local(): north, south = shifted('gx', v[0], v[rows - 1], False)]
    ppermute x12 -> x0, waiting for transfers between devices: 3.31 us -> none  [the longest x6 3.3 us: shifted(): lax.ppermute(first, axis, backward)]
    reduce_or x1 -> x0, other arithmetic: 2.79 us -> none  [local(): lit = jnp.any(slot_list[:, None] == jnp.arange(columns)[None, :], axis=0)]
    all_to_all x1, starting transfers between devices: 5.21 us -> 7.33 us  [local(): lax.all_to_all(slot_tags.reshape(tile_count, capacity), ('gx', 'gy'), spl...]
  transfers between devices with their start and end apart: 14 -> 2, of which waited for: 3 -> 1; matrix products, arithmetic and copies ran while one was open for 10% -> 5% of each run, Pallas kernels for 17% -> 55%
where the time goes in v2:
time: 184 us
  Pallas kernels  111 us (60%)
  waiting for transfers between devices  48.1 us (26%)
  starting transfers between devices  10.6 us (6%)
  local copies, waits for them, and re-layouts  9.78 us (5%)
  other arithmetic  3.49 us (2%)
    pallas_call x2, Pallas kernels, step(): pl.pallas_call(functools.partial(step_kernel, last), out_shape=outs, in_s...  53.8 us
    all_to_all x1, waiting for transfers between devices, local(): lax.all_to_all(packed, ('gx', 'gy'), split_axis=0, concat_axis=0, tiled=T...  48.1 us
    pallas_call x2, Pallas kernels, exchange(): pl.pallas_call(functools.partial(exchange_kernel, len(ins), nx, ny), out_...  28.7 us
    pallas_call x1, Pallas kernels, prep(): pl.pallas_call(functools.partial(prep_kernel, rows), out_shape=(jax.Shape...  11.1 us
    pallas_call x1, Pallas kernels, chem(): pl.pallas_call(chem_kernel, grid=(blocks // per,), out_shape=jax.ShapeDty...  9.65 us
    pallas_call x1, Pallas kernels, pack(): pl.pallas_call(pack_kernel, grid=(slots // tile,), out_shape=jax.ShapeDty...  7.94 us
    all_to_all x1, starting transfers between devices, local(): lax.all_to_all(slot_tags.reshape(tile_count, capacity), ('gx', 'gy'), spl...  7.33 us
  transfers between devices with their start and end apart: 2, of which 1 were waited for; matrix products, arithmetic and copies ran while one was open for 5% of the time, Pallas kernels for 55%

profile of v2, /device:TPU:0, one launch (start us, length us, event | category | flops | bytes accessed | tf_op | source)
XLA Modules:
  0.0 183.9 jit_solution(6972985085878600602)
XLA Ops:
  0.6 0.7 slice_add_fusion
  1.3 0.5 convert_reduce_fusion
  1.9 0.9 select_reduce_fusion
  2.8 0.7 sub.7
  3.5 7.3 %all-to-all-start.1 = ((s32[32,1,64]{2,1,0:T(1,128)}), s32[32,1,64]{2,1,0:T(1,128)S(1)}, u32[]{:S(2)}, u32[]{:S(2)}) async-start(s32[32,1,64]{2,1,0:T(1,128)} %sub.7), calls=%async_computation.1 | async-start | bytes 32768 | tf_op jit(solution)/shard_map/all_to_all | solution.py:473
  10.8 0.7 add_convert_fusion.flag_ref
  11.5 2.0 %copy.23.refs_5_ = s32[2048,1]{1,0:T(8,128)} copy(s32[2048,1]{0,1:T(1,128)} %bitcast.23) | data formatting | bytes 16384 | tf_op jit(solution)/shard_map/reshape | solution.py:449
  13.5 1.7 copy.21.refs_3_
  15.2 1.7 copy.22.refs_4_
  16.9 11.1 %prep.1 = (f32[16,512,128]{2,1,0:T(8,128)}, f32[16,128,128]{2,1,0:T(8,128)}, f32[16,128,128]{2,1,0:T(8,128)}, bf16[3,640,128]{2,1,0:T(8,128)(2,1)}) custom-call(f32[8192,128]{1,0:T(8,128)} %bitcast.17, f32[4096,128]{1,0:T(8,128)} %bitcast.18), custom_call_target="tpu_custom_call" | custom-call | tf_op jit(solution)/shard_map/prep/pallas_call | solution.py:63
  28.1 17.0 %exchange0.1 = (f32[4,640,128]{2,1,0:T(8,128)}, bf16[1024,512]{1,0:T(8,128)(2,1)}, bf16[1024,1024]{1,0:T(8,128)(2,1)}, bf16[512,1024]{1,0:T(8,128)(2,1)}, f32[10...) custom-call(bf16[3,640,128]{2,1,0:T(8,128)(2,1)} %get-tuple-element.20.rim_ref, ...), custom_call_target="tpu_custom_call" | custom-call | tf_op jit(solution)/shard_map/exchange0/pallas_call | solution.py:174
  45.1 27.2 %step_first.1 = (f32[16,512,128]{2,1,0:T(8,128)}, bf16[3,512,128]{2,1,0:T(8,128)(2,1)}) custom-call(f32[2]{0:T(128)} %add_convert_fusion.flag_ref, f32[16,512,128]{2,1,0:T(8,128)} %get-tuple-element.17.v_ref, f32[16,128,128]{2,1,0:T(8,128)} %get-tuple-element.18.lat_ref, f32[16,128,128]{2,1,0:T(8,128)} %get-tuple-element.19.lon_ref, ...), custom_call_target="tpu_custom_call" | custom-call | tf_op jit(solution)/shard_map/step_first/pallas_call | solution.py:324
  72.3 11.7 %exchange1.1.halo_ref = f32[4,512,128]{2,1,0:T(8,128)} custom-call(bf16[3,512,128]{2,1,0:T(8,128)(2,1)} %get-tuple-element.29.rim_ref), custom_call_target="tpu_custom_call" | custom-call | tf_op jit(solution)/shard_map/exchange1/pallas_call | solution.py:174
  83.9 0.2 broadcast_in_dim.19
  84.1 0.9 reshape_reshape.3.target_ref
  85.1 26.7 %step_last.1 = (f32[8192,128]{1,0:T(8,128)}, bf16[256,2048]{1,0:T(8,128)(2,1)}) custom-call(f32[2]{0:T(128)} %add_convert_fusion.flag_ref, f32[16,512,128]{2,1,0:T(8,128)} %get-tuple-element.28.v_ref, f32[16,128,128]{2,1,0:T(8,128)} %get-tuple-element.18.lat_ref, f32[16,128,128]{2,1,0:T(8,128)} %get-tuple-element.19.lon_ref, ...), custom_call_target="tpu_custom_call" | custom-call | tf_op jit(solution)/shard_map/step_last/pallas_call | solution.py:324
  111.7 7.9 %pack.1 = bf16[2048,512]{1,0:T(8,128)(2,1)} custom-call(bf16[256,2048]{1,0:T(8,128)(2,1)} %get-tuple-element.31.source_ref, s32[1,2048]{1,0:T(1,128)} %reshape_reshape.3.target_ref), custom_call_target="tpu_custom_call" | custom-call | tf_op jit(solution)/shard_map/pack/pallas_call | solution.py:356
  119.7 3.3 %all-to-all-start = ((bf16[32,64,512]{2,1,0:T(8,128)(2,1)}), bf16[32,64,512]{2,1,0:T(8,128)(2,1)S(1)}, u32[]{:S(2)}, u32[]{:S(2)}) async-start(bf16[32,64,512]{2,1,0:T(8,128)(2,1)} %bitcast.15), calls=%async_computation | async-start | bytes 4194304 | tf_op jit(solution)/shard_map/all_to_all | solution.py:486
  122.9 0.5 broadcast.29
  123.4 0.7 reduce.3
  124.1 0.7 reshape.81.tag_ref
  124.8 48.1 %all-to-all-done = bf16[32,64,512]{2,1,0:T(8,128)(2,1)S(1)} async-done(((bf16[32,64,512]{2,1,0:T(8,128)(2,1)}), bf16[32,64,512]{2,1,0:T(8,128)(2,1)S(1)}, u32[]{:S(2)}, u32[]{:S(2)}) %all-to-all-start) | async-done | bytes 2097184 | tf_op jit(solution)/shard_map/all_to_all | solution.py:486
  173.0 1.3 copy-done
  174.3 9.6 %chem.1 = bf16[2048,256]{1,0:T(8,128)(2,1)} custom-call(bf16[2048,512]{1,0:T(8,128)(2,1)} %bitcast.16, s32[1,2048]{1,0:T(1,128)} %reshape.81.tag_ref, bf16[16,128,128]{2,1,0:T(8,128)(2,1)} %bitcast.20, bf16[256,1024]{1,0:T(8,128)(2,1)} %w1_ref.1, f32[1,1024]{1,0:T(1,128)} %bitcast.27, bf16[1024,256]{1,0:T(8,128)(2,1)} %w2_ref.1), custom_call_target="tpu_custom_call" | custom-call | tf_op jit(solution)/shard_map/chem/pallas_call | solution.py:404
  (4 shorter events, 0.0 us)
Async XLA Ops:
  3.5 116.2 %all-to-all-start.1 = ((s32[32,1,64]{2,1,0:T(1,128)}), s32[32,1,64]{2,1,0:T(1,128)S(1)}, u32[]{:S(2)}, u32[]{:S(2)}) async-start(s32[32,1,64]{2,1,0:T(1,128)} %sub.7), calls=%async_computation.1 | async-start | bytes 32768 | tf_op jit(solution)/shard_map/all_to_all | solution.py:473
  119.7 53.3 %all-to-all-start = ((bf16[32,64,512]{2,1,0:T(8,128)(2,1)}), bf16[32,64,512]{2,1,0:T(8,128)(2,1)S(1)}, u32[]{:S(2)}, u32[]{:S(2)}) async-start(bf16[32,64,512]{2,1,0:T(8,128)(2,1)} %bitcast.15), calls=%async_computation | async-start | bytes 4194304 | tf_op jit(solution)/shard_map/all_to_all | solution.py:486
  173.0 1.3 copy-start

commit v3 on v2

--- a/solution.py
+++ b/solution.py
@@ -80,7 +80,7 @@
     ins, refs = refs[:extra], refs[extra:]
     halo_ref, refs = refs[0], refs[1:]
     outs, refs = refs[:extra], refs[extra:]
-    land_ref, send_sem, recv_sem = refs
+    land_ref, send_sem, recv_sem = refs[:3]
     gx, gy = lax.axis_index("gx"), lax.axis_index("gy")
     west, east = lax.rem(gy + ny - 1, ny), lax.rem(gy + 1, ny)
     barrier = pltpu.get_barrier_semaphore()
@@ -134,12 +134,14 @@
         for k in range(3):
             outs[k][...] = ins[k][...].T
         for k in range(3, 5):
-            outs[k][...] = jnp.broadcast_to(ins[k][...], outs[k].shape)
+            outs[k][...] = jnp.broadcast_to(ins[k][...], outs[k].shape[::-1]).T
         slots, lit_ref = ins[5], outs[5]
-        shape = (slots.shape[0], lit_ref.shape[2])
+        shape = (slots.shape[1], lit_ref.shape[2])
+        slot_rows = refs[3]
+        slot_rows[...] = jnp.broadcast_to(slots[...], shape[::-1]).T
 
         def mark(r, carry):
-            hit = slots[...] == lanes_of(shape) + r * shape[1]
+            hit = slot_rows[...] == lanes_of(shape) + r * shape[1]
             lit_ref[r] = jnp.max(jnp.where(hit, 1.0, 0.0), axis=0, keepdims=True)
             return carry
 
@@ -180,7 +182,8 @@
             pltpu.VMEM((4, depth, cols), jnp.bfloat16),
             pltpu.SemaphoreType.DMA((4,)),
             pltpu.SemaphoreType.DMA((4,)),
-        ],
+        ]
+        + ([pltpu.VMEM((ins[5].shape[1], cols), jnp.int32)] if ins else []),
         compiler_params=pltpu.CompilerParams(collective_id=number, has_side_effects=True),
         name="exchange%d" % number,
     )(rim, *ins)
@@ -206,14 +209,14 @@
     levels = lat_ref.shape[1]
     count = total // levels
     if last:
-        out_ref, src_ref, adv_ref, x_ref, one_ref, two_ref = refs
+        out_ref, src_ref, adv_a, adv_b, x_a, x_b, one_ref, two_ref = refs
     else:
-        out_ref, rim_ref, adv_ref, x_ref, one_ref, two_ref, edge_ref = refs
+        out_ref, rim_ref, adv_a, adv_b, x_a, x_b, one_ref, two_ref, edge_ref = refs
         edge_ref[...] = jnp.zeros_like(edge_ref)
     hidden = w1_ref.shape[0]
     lane = lanes_of((levels, width))
 
-    def advect_row(r, slot):
+    def advect_row(r, slot, adv_ref, x_ref):
         is_top = r == 0
         is_low = r == rows - 1
         up = jnp.maximum(r - 1, 0)
@@ -243,7 +246,8 @@
         g1 = 0.5 * (c + east_of(c, chalo_ref[3, chalo_ref.shape[1] - levels :, :]))
         gpos0, gneg0 = jnp.maximum(g0, 0.0), jnp.minimum(g0, 0.0)
         gpos1, gneg1 = jnp.maximum(g1, 0.0), jnp.minimum(g1, 0.0)
-        for f in range(count):
+
+        def one_field(f):
             part = slice(f * levels, (f + 1) * levels)
             v = v_ref[r, part, :]
             vn = jnp.where(is_top, halo_ref[0, part, :], v_ref[up, part, :])
@@ -258,18 +262,29 @@
             adv_ref[part, slot * width : (slot + 1) * width] = new
             x_ref[part, slot * width : (slot + 1) * width] = new.astype(jnp.bfloat16)
 
-    def body(i, carry):
+        return one_field
+
+    def advect_work(pair, adv_ref, x_ref):
         for k in range(GROUP):
-            advect_row(i * GROUP + k, k)
+            one_field = advect_row(pair * GROUP + k, k, adv_ref, x_ref)
+            for f in range(count):
+                one_field(f)
+                yield
+
+    def net(i, adv_ref, x_ref, work):
         chunk = 256
         for h in range(0, hidden, chunk):
             acc = jnp.dot(w1_ref[h : h + chunk, :], x_ref[...], preferred_element_type=jnp.float32)
+            next(work, None)
             bias = jnp.concatenate([b1_ref[h : h + chunk, :]] * GROUP, axis=1)
             one_ref[h : h + chunk, :] = silu(acc + bias).astype(jnp.bfloat16)
         for h in range(0, hidden, chunk):
             acc = jnp.dot(w2_ref[h : h + chunk, :], one_ref[...], preferred_element_type=jnp.float32)
+            next(work, None)
             bias = jnp.concatenate([b2_ref[h : h + chunk, :]] * GROUP, axis=1)
             two_ref[h : h + chunk, :] = silu(acc + bias).astype(jnp.bfloat16)
+        for _ in work:
+            pass
         lit = jnp.concatenate([lit_ref[i * GROUP + k] for k in range(GROUP)], axis=1)
         for h in range(0, total, chunk):
             heat = jnp.dot(w3_ref[h : h + chunk, :], two_ref[...], preferred_element_type=jnp.float32)
@@ -296,9 +311,18 @@
                             edge_ref[h : h + chunk, :],
                         ),
                     )
+
+    pairs = rows // GROUP
+
+    def body(i, carry):
+        net(2 * i, adv_a, x_a, advect_work(2 * i + 1, adv_b, x_b))
+        ahead = jnp.minimum(2 * i + 2, pairs - 1)
+        net(2 * i + 1, adv_b, x_b, advect_work(ahead, adv_a, x_a))
         return carry
 
-    lax.fori_loop(0, rows // GROUP, body, 0)
+    for _ in advect_work(0, adv_a, x_a):
+        pass
+    lax.fori_loop(0, pairs // 2, body, 0)
     if not last:
         rim_ref[0] = out_ref[0].astype(jnp.bfloat16)
         rim_ref[1] = out_ref[rows - 1].astype(jnp.bfloat16)
@@ -328,6 +352,8 @@
         out_specs=(VMEM,) * 2,
         scratch_shapes=[
             pltpu.VMEM((total, wide), f32),
+            pltpu.VMEM((total, wide), f32),
+            pltpu.VMEM((total, wide), bf16),
             pltpu.VMEM((total, wide), bf16),
             pltpu.VMEM((hidden, wide), bf16),
             pltpu.VMEM((hidden, wide), bf16),
@@ -337,33 +363,115 @@
     )(flags, v, lat, lon, halo, chalo, lit, *nets)
 
 
-def pack_kernel(source_ref, target_ref, out_ref):
-    tile = out_ref.shape[0]
+def route_kernel(
+    ny, groups, source_ref, target_ref, tag_ref, out_ref, tag_out, send_ref, sems, tag_sems
+):
+    tiles, capacity, _ = out_ref.shape
     feats, cols = source_ref.shape
-    slot = lax.broadcasted_iota(jnp.int32, (tile, cols), 0) + pl.program_id(0) * tile
-    lane = lanes_of((tile, cols))
-    match = slot == target_ref[...]
-    for c in range(SEG):
-        hit = (match & (lane % SEG == c)).astype(jnp.float32).astype(jnp.bfloat16)
-        out_ref[:, c * feats : (c + 1) * feats] = lax.dot_general(
-            hit, source_ref[...], (((1,), (1,)), ((), ())), preferred_element_type=jnp.float32
-        ).astype(jnp.bfloat16)
-
-
-def pack(source, target, slots):
+    per = tiles // groups
+    me = lax.axis_index("gx") * ny + lax.axis_index("gy")
+    barrier = pltpu.get_barrier_semaphore()
+    mesh_id = pl.DeviceIdType.MESH
+
+    def place(tile):
+        return (lax.div(tile, ny), lax.rem(tile, ny))
+
+    def greet(k, carry):
+        pl.semaphore_signal(
+            barrier, inc=1, device_id=place(lax.rem(me + k, tiles)), device_id_type=mesh_id
+        )
+        return carry
+
+    lax.fori_loop(1, tiles, greet, 0)
+    tile = per * capacity
+    slot = lax.broadcasted_iota(jnp.int32, (tile, cols), 0)
+    lane = lanes_of((1, cols))
+    own = lax.div(me, per)
+
+    def pack(j):
+        group = lax.rem(own + j, groups)
+        target = target_ref[...] - group * tile
+        for c in range(SEG):
+            wanted = jnp.where(lane % SEG == c, target, -1)
+            hit = (slot == wanted).astype(jnp.float32).astype(jnp.bfloat16)
+            packed = lax.dot_general(
+                hit, source_ref[...], (((1,), (1,)), ((), ())), preferred_element_type=jnp.float32
+            ).astype(jnp.bfloat16)
+            send_ref[pl.ds(group * per, per), :, c * feats : (c + 1) * feats] = packed.reshape(
+                per, capacity, feats
+            )
+
+    def copies(peer, landing):
+        common = dict(device_id=place(peer), device_id_type=mesh_id)
+        return (
+            pltpu.make_async_remote_copy(
+                src_ref=send_ref.at[peer],
+                dst_ref=out_ref.at[landing],
+                send_sem=sems.at[0, peer],
+                recv_sem=sems.at[1, landing],
+                **common,
+            ),
+            pltpu.make_async_remote_copy(
+                src_ref=tag_ref.at[peer],
+                dst_ref=tag_out.at[landing],
+                send_sem=tag_sems.at[0, peer],
+                recv_sem=tag_sems.at[1, landing],
+                **common,
+            ),
+        )
+
+    def launch(j):
+        group = lax.rem(own + j, groups)
+        for k in range(per):
+            peer = group * per + k
+
+            @pl.when(peer != me)
+            def _():
+                for copy in copies(peer, me):
+                    copy.start()
+
+    pack(groups // 2)
+    pl.semaphore_wait(barrier, tiles - 1)
+
+    def body(j, carry):
+        pack(lax.rem(groups // 2 + j, groups))
+        launch(lax.rem(groups // 2 + j - 1, groups))
+        return carry
+
+    lax.fori_loop(1, groups, body, 0)
+    launch(groups // 2 - 1)
+    out_ref[me] = send_ref[me]
+    tag_out[me] = tag_ref[me]
+
+    def finish(k, carry):
+        peer = lax.rem(me + k, tiles)
+        for copy in copies(peer, peer):
+            copy.wait()
+        return carry
+
+    lax.fori_loop(1, tiles, finish, 0)
+
+
+def route(source, target, tags):
     feats, cols = source.shape
-    tile = 256
+    tiles, _, capacity = tags.shape
+    bf16 = jnp.bfloat16
     return pl.pallas_call(
-        pack_kernel,
-        grid=(slots // tile,),
-        out_shape=jax.ShapeDtypeStruct((slots, SEG * feats), jnp.bfloat16),
-        in_specs=[
-            pl.BlockSpec((feats, cols), lambda i: (0, 0)),
-            pl.BlockSpec((1, cols), lambda i: (0, 0)),
+        functools.partial(route_kernel, lax.axis_size("gy"), 8),
+        out_shape=(
+            jax.ShapeDtypeStruct((tiles, capacity, SEG * feats), bf16),
+            jax.ShapeDtypeStruct((tiles, 1, capacity), jnp.int32),
+        ),
+        in_specs=[VMEM] * 3,
+        out_specs=(VMEM,) * 2,
+        scratch_shapes=[
+            pltpu.VMEM((tiles, capacity, SEG * feats), bf16),
+            pltpu.SemaphoreType.DMA((2, tiles)),
+            pltpu.SemaphoreType.DMA((2, tiles)),
         ],
-        out_specs=pl.BlockSpec((tile, SEG * feats), lambda i: (i, 0)),
-        name="pack",
-    )(source, target)
+        compiler_params=pltpu.CompilerParams(collective_id=7, has_side_effects=True),
+        name="route",
+    )(source, target, tags)
 
 
 def chem_kernel(arrived_ref, tag_ref, regrid_ref, w1_ref, b1_ref, w2_ref, out_ref, cell_ref):
@@ -444,13 +552,13 @@
         rad_w1,
         rad_w2,
         rad_w3,
-        rad_b1.reshape(-1, 1),
-        rad_b2.reshape(-1, 1),
-        sun_columns.reshape(-1, 1),
+        rad_b1.reshape(1, -1),
+        rad_b2.reshape(1, -1),
+        sun_columns.reshape(1, -1),
     )
     shapes = (
         *(jax.ShapeDtypeStruct(w.shape[::-1], bf16) for w in ins[:3]),
-        *(jax.ShapeDtypeStruct((b.shape[0], cols), f32) for b in ins[3:5]),
+        *(jax.ShapeDtypeStruct((b.shape[1], cols), f32) for b in ins[3:5]),
         jax.ShapeDtypeStruct((rows, 1, cols), f32),
     )
     chalo, w1, w2, w3, b1, b2, lit = exchange(rim, 0, ins, shapes)
@@ -470,9 +578,7 @@
     target_row = destination * capacity + order_rank
     placement = target_row[None, :] == jnp.arange(slots)[:, None]
     slot_tags = jnp.sum(jnp.where(placement, arrival_slot[None, :] + 1, 0), axis=1) - 1
-    tags = lax.all_to_all(
-        slot_tags.reshape(tile_count, capacity), ("gx", "gy"), split_axis=0, concat_axis=0, tiled=True
-    ).reshape(1, slots)
+    slot_tags = slot_tags.reshape(tile_count, 1, capacity)
     column_target = jnp.repeat(target_row, SEG).reshape(1, columns)
 
     halo = chalo
@@ -482,9 +588,9 @@
         if not last:
             (halo,) = exchange(rim, repeat + 1, (), ())
     source = rim
-    packed = pack(source, column_target, slots).reshape(tile_count, capacity, SEG * 2 * levels)
-    arrived = lax.all_to_all(packed, ("gx", "gy"), split_axis=0, concat_axis=0, tiled=True)
+    arrived, tags = route(source, column_target, slot_tags)
     arrived = arrived.reshape(slots, SEG * 2 * levels)
+    tags = tags.reshape(1, slots)
     output = chem(arrived, tags, regrid_weights[0, 0], chem_w1, chem_b1.reshape(1, -1), chem_w2)
     return (
         v.reshape(field_count, levels, rows, cols),

time: 184 us -> 162 us (0.88)
  the two profiles are of different devices: /device:TPU:0 before, /device:TPU:25 now
where the time goes in v3:
time: 162 us
  Pallas kernels  155 us (96%)
  other arithmetic  3.42 us (2%)
  local copies, waits for them, and re-layouts  2.99 us (2%)
    pallas_call x1, Pallas kernels, route(): pl.pallas_call(functools.partial(route_kernel, lax.axis_size('gy'), 8), o...  61.4 us
    pallas_call x2, Pallas kernels, step(): pl.pallas_call(functools.partial(step_kernel, last), out_shape=outs, in_s...  45.9 us
    pallas_call x2, Pallas kernels, exchange(): pl.pallas_call(functools.partial(exchange_kernel, len(ins), nx, ny), out_...  26.8 us
    pallas_call x1, Pallas kernels, prep(): pl.pallas_call(functools.partial(prep_kernel, rows), out_shape=(jax.Shape...  11.1 us
    pallas_call x1, Pallas kernels, chem(): pl.pallas_call(chem_kernel, grid=(blocks // per,), out_shape=jax.ShapeDty...  9.66 us

profile of v3, /device:TPU:25, one launch (start us, length us, event | category | flops | bytes accessed | tf_op | source)
XLA Modules:
  0.0 161.9 jit_solution(18009740830753562994)
XLA Ops:
  0.6 11.1 %prep.1 = (f32[16,512,128]{2,1,0:T(8,128)}, f32[16,128,128]{2,1,0:T(8,128)}, f32[16,128,128]{2,1,0:T(8,128)}, bf16[3,640,128]{2,1,0:T(8,128)(2,1)}) custom-call(f32[8192,128]{1,0:T(8,128)} %bitcast.14, f32[4096,128]{1,0:T(8,128)} %bitcast.15), custom_call_target="tpu_custom_call" | custom-call | tf_op jit(solution)/shard_map/prep/pallas_call | solution.py:63
  11.8 14.8 %exchange0.1 = (f32[4,640,128]{2,1,0:T(8,128)}, bf16[1024,512]{1,0:T(8,128)(2,1)}, bf16[1024,1024]{1,0:T(8,128)(2,1)}, bf16[512,1024]{1,0:T(8,128)(2,1)}, f32[10...) custom-call(bf16[3,640,128]{2,1,0:T(8,128)(2,1)} %get-tuple-element.22.rim_ref, ...), custom_call_target="tpu_custom_call" | custom-call | tf_op jit(solution)/shard_map/exchange0/pallas_call | solution.py:176
  26.6 0.6 add_convert_fusion.flag_ref
  27.2 22.8 %step_first.1 = (f32[16,512,128]{2,1,0:T(8,128)}, bf16[3,512,128]{2,1,0:T(8,128)(2,1)}) custom-call(f32[2]{0:T(128)} %add_convert_fusion.flag_ref, f32[16,512,128]{2,1,0:T(8,128)} %get-tuple-element.19.v_ref, f32[16,128,128]{2,1,0:T(8,128)} %get-tuple-element.20.lat_ref, f32[16,128,128]{2,1,0:T(8,128)} %get-tuple-element.21.lon_ref, ...), custom_call_target="tpu_custom_call" | custom-call | tf_op jit(solution)/shard_map/step_first/pallas_call | solution.py:348
  50.0 12.0 %exchange1.1.halo_ref = f32[4,512,128]{2,1,0:T(8,128)} custom-call(bf16[3,512,128]{2,1,0:T(8,128)(2,1)} %get-tuple-element.31.rim_ref), custom_call_target="tpu_custom_call" | custom-call | tf_op jit(solution)/shard_map/exchange1/pallas_call | solution.py:176
  61.9 0.0 copy-start
  61.9 23.1 %step_last.1 = (f32[8192,128]{1,0:T(8,128)}, bf16[256,2048]{1,0:T(8,128)(2,1)}) custom-call(f32[2]{0:T(128)} %add_convert_fusion.flag_ref, f32[16,512,128]{2,1,0:T(8,128)} %get-tuple-element.30.v_ref, f32[16,128,128]{2,1,0:T(8,128)} %get-tuple-element.20.lat_ref, f32[16,128,128]{2,1,0:T(8,128)} %get-tuple-element.21.lon_ref, ...), custom_call_target="tpu_custom_call" | custom-call | tf_op jit(solution)/shard_map/step_last/pallas_call | solution.py:348
  85.0 0.0 copy-done
  85.0 0.5 convert_reduce_fusion
  85.6 0.9 select_reduce_fusion
  86.5 0.7 sub.7.tag_ref
  87.2 0.2 broadcast_in_dim.19
  87.4 0.9 reshape_reshape.3.target_ref
  88.3 61.4 %route.1 = (bf16[32,64,512]{2,1,0:T(8,128)(2,1)}, s32[32,1,64]{2,1,0:T(1,128)}) custom-call(bf16[256,2048]{1,0:T(8,128)(2,1)} %get-tuple-element.33.source_ref, s32[1,2048]{1,0:T(1,128)} %reshape_reshape.3.target_ref, s32[32,1,64]{2,1,0:T(1,128)} %sub.7.tag_ref), custom_call_target="tpu_custom_call" | custom-call | tf_op jit(solution)/shard_map/route/pallas_call | solution.py:459
  149.7 0.5 broadcast.28
  150.2 1.4 reduce.3
  151.6 0.7 reshape.73.tag_ref
  152.3 9.7 %chem.1 = bf16[2048,256]{1,0:T(8,128)(2,1)} custom-call(bf16[2048,512]{1,0:T(8,128)(2,1)} %bitcast.16, s32[1,2048]{1,0:T(1,128)} %reshape.73.tag_ref, bf16[16,128,128]{2,1,0:T(8,128)(2,1)} %bitcast.18, bf16[256,1024]{1,0:T(8,128)(2,1)} %w1_ref.1, f32[1,1024]{1,0:T(1,128)} %bitcast.25, bf16[1024,256]{1,0:T(8,128)(2,1)} %w2_ref.1), custom_call_target="tpu_custom_call" | custom-call | tf_op jit(solution)/shard_map/chem/pallas_call | solution.py:512
  (3 shorter events, 0.0 us)
Async XLA Ops:
  61.9 23.1 %copy-start = (s32[2,1,1,1024]{3,2,1,0:T(1,128)S(1)}, s32[2,1,1,1024]{3,2,1,0:T(1,128)}, u32[]{:S(2)}) copy-start(s32[2,1,1,1024]{3,2,1,0:T(1,128)} %param.21) | copy-start | bytes 24580

commit v4 on v3

--- a/solution.py
+++ b/solution.py
@@ -24,6 +24,11 @@
     return lax.broadcasted_iota(jnp.int32, shape, len(shape) - 1)
 
 
+def edge_lanes(lane, r):
+    width = lane.shape[-1]
+    return (lane == 2 * r) | (lane == lax.rem(2 * r + width - 1, width))
+
+
 def prep_kernel(rows, f_ref, c_ref, v_ref, lat_ref, lon_ref, rim_ref, edge_ref):
     total = f_ref.shape[0] // rows
     levels = lat_ref.shape[1]
@@ -32,11 +37,7 @@
     def edges(part, value, r):
         lane = lanes_of(value.shape)
         edge_ref[part, :] = jnp.where(
-            lane == r,
-            pltpu.roll(value, r, axis=1),
-            jnp.where(
-                lane == rows + r, pltpu.roll(value, rows + 1 + r, axis=1), edge_ref[part, :]
-            ),
+            edge_lanes(lane, r), pltpu.roll(value, 2 * r, axis=1), edge_ref[part, :]
         )
 
     def body(r, carry):
@@ -75,12 +76,7 @@
     )(fields.reshape(total * rows, cols), courant.reshape(2 * levels * rows, cols))
 
 
-def exchange_kernel(extra, nx, ny, rim_ref, *refs):
-    refs = list(refs)
-    ins, refs = refs[:extra], refs[extra:]
-    halo_ref, refs = refs[0], refs[1:]
-    outs, refs = refs[:extra], refs[extra:]
-    land_ref, send_sem, recv_sem = refs[:3]
+def swap_halos(nx, ny, rim_ref, land_ref, send_sem, recv_sem):
     gx, gy = lax.axis_index("gx"), lax.axis_index("gy")
     west, east = lax.rem(gy + ny - 1, ny), lax.rem(gy + 1, ny)
     barrier = pltpu.get_barrier_semaphore()
@@ -89,21 +85,6 @@
 
     def greet(target):
         pl.semaphore_signal(barrier, inc=1, device_id=target, device_id_type=mesh_id)
-
-    land_ref[0] = jnp.zeros_like(land_ref[0])
-    land_ref[1] = jnp.zeros_like(land_ref[1])
-    greet((gx, west))
-    greet((gx, east))
-
-    @pl.when(has_north)
-    def _():
-        greet((gx - 1, gy))
-
-    @pl.when(has_south)
-    def _():
-        greet((gx + 1, gy))
-
-    pl.semaphore_wait(barrier, 2 + jnp.minimum(gx, 1) + jnp.minimum(nx - 1 - gx, 1))
 
     def copy(source, slot, target):
         return pltpu.make_async_remote_copy(
@@ -120,16 +101,73 @@
     to_east = copy(2, 2, (gx, east))
     to_west = copy(2, 3, (gx, west))
 
-    @pl.when(has_south)
-    def _():
-        to_south.start()
-
-    @pl.when(has_north)
-    def _():
-        to_north.start()
-
-    to_east.start()
-    to_west.start()
+
+    def enter():
+        land_ref[0] = jnp.zeros_like(land_ref[0])
+        land_ref[1] = jnp.zeros_like(land_ref[1])
+        greet((gx, west))
+        greet((gx, east))
+
+        @pl.when(has_north)
+        def _():
+            greet((gx - 1, gy))
+
+        @pl.when(has_south)
+        def _():
+            greet((gx + 1, gy))
+
+    def ready():
+        pl.semaphore_wait(barrier, 2 + jnp.minimum(gx, 1) + jnp.minimum(nx - 1 - gx, 1))
+
+    def send_rows():
+        @pl.when(has_south)
+        def _():
+            to_south.start()
+
+        @pl.when(has_north)
+        def _():
+            to_north.start()
+
+    def send_edges():
+        to_east.start()
+        to_west.start()
+
+    def finish():
+        @pl.when(has_south)
+        def _():
+            to_south.wait_send()
+
+        @pl.when(has_north)
+        def _():
+            to_north.wait_send()
+
+        to_east.wait()
+        to_west.wait()
+
+        @pl.when(has_north)
+        def _():
+            to_south.wait_recv()
+
+        @pl.when(has_south)
+        def _():
+            to_north.wait_recv()
+
+    return enter, ready, send_rows, send_edges, finish
+
+
+def exchange_kernel(extra, nx, ny, rim_ref, *refs):
+    refs = list(refs)
+    ins, refs = refs[:extra], refs[extra:]
+    halo_ref, refs = refs[0], refs[1:]
+    outs, refs = refs[:extra], refs[extra:]
+    land_ref, send_sem, recv_sem = refs[:3]
+    enter, ready, send_rows, send_edges, finish = swap_halos(
+        nx, ny, rim_ref, land_ref, send_sem, recv_sem
+    )
+    enter()
+    ready()
+    send_rows()
+    send_edges()
     if extra:
         for k in range(3):
             outs[k][...] = ins[k][...].T
@@ -147,25 +185,7 @@
 
         lax.fori_loop(0, lit_ref.shape[0], mark, 0)
 
-    @pl.when(has_south)
-    def _():
-        to_south.wait_send()
-
-    @pl.when(has_north)
-    def _():
-        to_north.wait_send()
-
-    to_east.wait()
-    to_west.wait()
-
-    @pl.when(has_north)
-    def _():
-        to_south.wait_recv()
-
-    @pl.when(has_south)
-    def _():
-        to_north.wait_recv()
-
+    finish()
     for k in range(4):
         halo_ref[k] = land_ref[k].astype(jnp.float32)
 
@@ -191,6 +211,8 @@
 
 def step_kernel(
     last,
+    nx,
+    ny,
     flag_ref,
     v_ref,
     lat_ref,
@@ -211,7 +233,12 @@
     if last:
         out_ref, src_ref, adv_a, adv_b, x_a, x_b, one_ref, two_ref = refs
     else:
-        out_ref, rim_ref, adv_a, adv_b, x_a, x_b, one_ref, two_ref, edge_ref = refs
+        out_ref, next_ref, adv_a, adv_b, x_a, x_b, one_ref, two_ref, *refs = refs
+        edge_ref, rim_ref, land_ref, send_sem, recv_sem = refs
+        enter, ready, send_rows, send_edges, finish = swap_halos(
+            nx, ny, rim_ref, land_ref, send_sem, recv_sem
+        )
+        enter()
         edge_ref[...] = jnp.zeros_like(edge_ref)
     hidden = w1_ref.shape[0]
     lane = lanes_of((levels, width))
@@ -231,13 +258,13 @@
 
         def west_of(value, halo):
             return jnp.where(
-                lane == 0, pltpu.roll(halo, width - rows - r, axis=1), pltpu.roll(value, 1, axis=1)
+                lane == 0, pltpu.roll(halo, lax.rem(width + 1 - 2 * r, width), axis=1), pltpu.roll(value, 1, axis=1)
             )
 
         def east_of(value, halo):
             return jnp.where(
                 lane == width - 1,
-                pltpu.roll(halo, width - 1 - r, axis=1),
+                pltpu.roll(halo, width - 1 - 2 * r, axis=1),
                 pltpu.roll(value, width - 1, axis=1),
             )
 
@@ -303,30 +330,39 @@
                     out_ref[r, h : h + chunk, :] = piece
                     at = lanes_of(piece.shape)
                     edge_ref[h : h + chunk, :] = jnp.where(
-                        at == r,
-                        pltpu.roll(piece, r, axis=1),
-                        jnp.where(
-                            at == rows + r,
-                            pltpu.roll(piece, rows + 1 + r, axis=1),
-                            edge_ref[h : h + chunk, :],
-                        ),
+                        edge_lanes(at, r),
+                        pltpu.roll(piece, 2 * r, axis=1),
+                        edge_ref[h : h + chunk, :],
                     )
 
     pairs = rows // GROUP
 
+    def order(k):
+        return jnp.where(k == 0, 0, jnp.where(k == 1, pairs - 1, jnp.minimum(k - 1, pairs - 2)))
+
     def body(i, carry):
-        net(2 * i, adv_a, x_a, advect_work(2 * i + 1, adv_b, x_b))
-        ahead = jnp.minimum(2 * i + 2, pairs - 1)
-        net(2 * i + 1, adv_b, x_b, advect_work(ahead, adv_a, x_a))
+        net(order(2 * i), adv_a, x_a, advect_work(order(2 * i + 1), adv_b, x_b))
+        net(order(2 * i + 1), adv_b, x_b, advect_work(order(2 * i + 2), adv_a, x_a))
+        if not last:
+
+            @pl.when(i == 0)
+            def _():
+                rim_ref[0] = out_ref[0].astype(jnp.bfloat16)
+                rim_ref[1] = out_ref[rows - 1].astype(jnp.bfloat16)
+                ready()
+                send_rows()
+
         return carry
 
     for _ in advect_work(0, adv_a, x_a):
         pass
     lax.fori_loop(0, pairs // 2, body, 0)
     if not last:
-        rim_ref[0] = out_ref[0].astype(jnp.bfloat16)
-        rim_ref[1] = out_ref[rows - 1].astype(jnp.bfloat16)
         rim_ref[2] = edge_ref[...].astype(jnp.bfloat16)
+        send_edges()
+        finish()
+        for k in range(4):
+            next_ref[k] = land_ref[k].astype(jnp.float32)
 
 
 def step(last, flags, v, lat, lon, halo, chalo, lit, nets):
@@ -342,11 +378,11 @@
     else:
         outs = (
             jax.ShapeDtypeStruct((rows, total, cols), f32),
-            jax.ShapeDtypeStruct((3, total, cols), bf16),
+            jax.ShapeDtypeStruct((4, total, cols), f32),
         )
     wide = GROUP * cols
     return pl.pallas_call(
-        functools.partial(step_kernel, last),
+        functools.partial(step_kernel, last, lax.axis_size("gx"), lax.axis_size("gy")),
         out_shape=outs,
         in_specs=[SMEM] + [VMEM] * 11,
         out_specs=(VMEM,) * 2,
@@ -358,7 +394,20 @@
             pltpu.VMEM((hidden, wide), bf16),
             pltpu.VMEM((hidden, wide), bf16),
         ]
-        + ([] if last else [pltpu.VMEM((total, cols), f32)]),
+        + (
+            []
+            if last
+            else [
+                pltpu.VMEM((total, cols), f32),
+                pltpu.VMEM((3, total, cols), bf16),
+                pltpu.VMEM((4, total, cols), bf16),
+                pltpu.SemaphoreType.DMA((4,)),
+                pltpu.SemaphoreType.DMA((4,)),
+            ]
+        ),
+        compiler_params=None
+        if last
+        else pltpu.CompilerParams(collective_id=1, has_side_effects=True),
         name="step_last" if last else "step_first",
     )(flags, v, lat, lon, halo, chalo, lit, *nets)
 
@@ -584,10 +633,8 @@
     halo = chalo
     for repeat in range(STEPS):
         last = repeat == STEPS - 1
-        v, rim = step(last, flags, v, lat, lon, halo, chalo, lit, nets)
-        if not last:
-            (halo,) = exchange(rim, repeat + 1, (), ())
-    source = rim
+        v, halo = step(last, flags, v, lat, lon, halo, chalo, lit, nets)
+    source = halo
     arrived, tags = route(source, column_target, slot_tags)
     arrived = arrived.reshape(slots, SEG * 2 * levels)
     tags = tags.reshape(1, slots)

time: 162 us -> 154 us (0.951)
  Pallas kernels: 155 us -> 147 us
    pallas_call x2 -> x1, Pallas kernels: 26.8 us -> 14.8 us  [exchange(): pl.pallas_call(functools.partial(exchange_kernel, len(ins), nx, ny), out_...]
    pallas_call x2, Pallas kernels: 45.9 us -> 50.6 us  [step(): pl.pallas_call(functools.partial(step_kernel, last, lax.axis_size('gx'),...]
where the time goes in v4:
time: 154 us
  Pallas kernels  147 us (95%)
  other arithmetic  3.42 us (2%)
  local copies, waits for them, and re-layouts  2.99 us (2%)
    pallas_call x1, Pallas kernels, route(): pl.pallas_call(functools.partial(route_kernel, lax.axis_size('gy'), 8), o...  61.3 us
    pallas_call x2, Pallas kernels, step(): pl.pallas_call(functools.partial(step_kernel, last, lax.axis_size('gx'),...  50.6 us
    pallas_call x1, Pallas kernels, exchange(): pl.pallas_call(functools.partial(exchange_kernel, len(ins), nx, ny), out_...  14.8 us
    pallas_call x1, Pallas kernels, prep(): pl.pallas_call(functools.partial(prep_kernel, rows), out_shape=(jax.Shape...  10.1 us
    pallas_call x1, Pallas kernels, chem(): pl.pallas_call(chem_kernel, grid=(blocks // per,), out_shape=jax.ShapeDty...  9.65 us

profile of v4, /device:TPU:25, one launch (start us, length us, event | category | flops | bytes accessed | tf_op | source)
XLA Modules:
  0.0 153.6 jit_solution(7242167749489300274)
XLA Ops:
  0.6 10.1 %prep.1 = (f32[16,512,128]{2,1,0:T(8,128)}, f32[16,128,128]{2,1,0:T(8,128)}, f32[16,128,128]{2,1,0:T(8,128)}, bf16[3,640,128]{2,1,0:T(8,128)(2,1)}) custom-call(f32[8192,128]{1,0:T(8,128)} %bitcast.14, f32[4096,128]{1,0:T(8,128)} %bitcast.15), custom_call_target="tpu_custom_call" | custom-call | tf_op jit(solution)/shard_map/prep/pallas_call | solution.py:64
  10.8 14.8 %exchange0.1 = (f32[4,640,128]{2,1,0:T(8,128)}, bf16[1024,512]{1,0:T(8,128)(2,1)}, bf16[1024,1024]{1,0:T(8,128)(2,1)}, bf16[512,1024]{1,0:T(8,128)(2,1)}, f32[10...) custom-call(bf16[3,640,128]{2,1,0:T(8,128)(2,1)} %get-tuple-element.22.rim_ref, ...), custom_call_target="tpu_custom_call" | custom-call | tf_op jit(solution)/shard_map/exchange0/pallas_call | solution.py:196
  25.6 0.6 add_convert_fusion.flag_ref
  26.2 27.5 %step_first.1 = (f32[16,512,128]{2,1,0:T(8,128)}, f32[4,512,128]{2,1,0:T(8,128)}) custom-call(f32[2]{0:T(128)} %add_convert_fusion.flag_ref, f32[16,512,128]{2,1,0:T(8,128)} %get-tuple-element.19.v_ref, f32[16,128,128]{2,1,0:T(8,128)} %get-tuple-element.20.lat_ref, f32[16,128,128]{2,1,0:T(8,128)} %get-tuple-element.21.lon_ref, ...), custom_call_target="tpu_custom_call" | custom-call | tf_op jit(solution)/shard_map/step_first/pallas_call | solution.py:384
  53.6 0.0 copy-start
  53.7 23.2 %step_last.1 = (f32[8192,128]{1,0:T(8,128)}, bf16[256,2048]{1,0:T(8,128)(2,1)}) custom-call(f32[2]{0:T(128)} %add_convert_fusion.flag_ref, f32[16,512,128]{2,1,0:T(8,128)} %get-tuple-element.30.v_ref, f32[16,128,128]{2,1,0:T(8,128)} %get-tuple-element.20.lat_ref, f32[16,128,128]{2,1,0:T(8,128)} %get-tuple-element.21.lon_ref, ...), custom_call_target="tpu_custom_call" | custom-call | tf_op jit(solution)/shard_map/step_last/pallas_call | solution.py:384
  76.8 0.0 copy-done
  76.8 0.5 convert_reduce_fusion
  77.3 0.9 select_reduce_fusion
  78.3 0.7 sub.7.tag_ref
  79.0 0.2 broadcast_in_dim.19
  79.2 0.9 reshape_reshape.3.target_ref
  80.1 61.3 %route.1 = (bf16[32,64,512]{2,1,0:T(8,128)(2,1)}, s32[32,1,64]{2,1,0:T(1,128)}) custom-call(bf16[256,2048]{1,0:T(8,128)(2,1)} %get-tuple-element.33.source_ref, s32[1,2048]{1,0:T(1,128)} %reshape_reshape.3.target_ref, s32[32,1,64]{2,1,0:T(1,128)} %sub.7.tag_ref), custom_call_target="tpu_custom_call" | custom-call | tf_op jit(solution)/shard_map/route/pallas_call | solution.py:508
  141.4 0.5 broadcast.28
  141.9 1.4 reduce.3
  143.3 0.7 reshape.73.tag_ref
  144.0 9.7 %chem.1 = bf16[2048,256]{1,0:T(8,128)(2,1)} custom-call(bf16[2048,512]{1,0:T(8,128)(2,1)} %bitcast.16, s32[1,2048]{1,0:T(1,128)} %reshape.73.tag_ref, bf16[16,128,128]{2,1,0:T(8,128)(2,1)} %bitcast.18, bf16[256,1024]{1,0:T(8,128)(2,1)} %w1_ref.1, f32[1,1024]{1,0:T(1,128)} %bitcast.25, bf16[1024,256]{1,0:T(8,128)(2,1)} %w2_ref.1), custom_call_target="tpu_custom_call" | custom-call | tf_op jit(solution)/shard_map/chem/pallas_call | solution.py:561
  (3 shorter events, 0.0 us)
Async XLA Ops:
  53.6 23.2 %copy-start = (s32[2,1,1,1024]{3,2,1,0:T(1,128)S(1)}, s32[2,1,1,1024]{3,2,1,0:T(1,128)}, u32[]{:S(2)}) copy-start(s32[2,1,1,1024]{3,2,1,0:T(1,128)} %param.21) | copy-start | bytes 24580

commit v5 on v4

--- a/solution.py
+++ b/solution.py
@@ -29,9 +29,13 @@
     return (lane == 2 * r) | (lane == lax.rem(2 * r + width - 1, width))
 
 
-def prep_kernel(rows, f_ref, c_ref, v_ref, lat_ref, lon_ref, rim_ref, edge_ref):
+def prep_kernel(rows, f_ref, c_ref, v_ref, lat_ref, lon_ref, rim_ref, edge_ref, send_rows):
     total = f_ref.shape[0] // rows
     levels = lat_ref.shape[1]
+    for k, r in enumerate((0, rows - 1)):
+        rim_ref[k, :total, :] = f_ref[pl.ds(r, total, stride=rows), :].astype(jnp.bfloat16)
+        rim_ref[k, total:, :] = c_ref[pl.ds(r, levels, stride=rows), :].astype(jnp.bfloat16)
+    send_rows()
     edge_ref[...] = jnp.zeros_like(edge_ref)
 
     def edges(part, value, r):
@@ -51,29 +55,7 @@
         return carry
 
     lax.fori_loop(0, rows, body, 0)
-    for k, r in enumerate((0, rows - 1)):
-        rim_ref[k, :total, :] = v_ref[r].astype(jnp.bfloat16)
-        rim_ref[k, total:, :] = lat_ref[r].astype(jnp.bfloat16)
     rim_ref[2] = edge_ref[...].astype(jnp.bfloat16)
-
-
-def prep(fields, courant):
-    count, levels, rows, cols = fields.shape
-    total = count * levels
-    f32 = jnp.float32
-    return pl.pallas_call(
-        functools.partial(prep_kernel, rows),
-        out_shape=(
-            jax.ShapeDtypeStruct((rows, total, cols), f32),
-            jax.ShapeDtypeStruct((rows, levels, cols), f32),
-            jax.ShapeDtypeStruct((rows, levels, cols), f32),
-            jax.ShapeDtypeStruct((3, total + levels, cols), jnp.bfloat16),
-        ),
-        in_specs=[VMEM, VMEM],
-        out_specs=(VMEM,) * 4,
-        scratch_shapes=[pltpu.VMEM((total + levels, cols), f32)],
-        name="prep",
-    )(fields.reshape(total * rows, cols), courant.reshape(2 * levels * rows, cols))
 
 
 def swap_halos(nx, ny, rim_ref, land_ref, send_sem, recv_sem):
@@ -155,58 +137,73 @@
     return enter, ready, send_rows, send_edges, finish
 
 
-def exchange_kernel(extra, nx, ny, rim_ref, *refs):
-    refs = list(refs)
-    ins, refs = refs[:extra], refs[extra:]
-    halo_ref, refs = refs[0], refs[1:]
-    outs, refs = refs[:extra], refs[extra:]
-    land_ref, send_sem, recv_sem = refs[:3]
+def exchange_kernel(rows, nx, ny, *refs):
+    f_ref, c_ref, *ins = refs[:8]
+    halo_ref, v_ref, lat_ref, lon_ref, *outs = refs[8:18]
+    rim_ref, edge_ref, land_ref, send_sem, recv_sem, slot_rows = refs[18:]
     enter, ready, send_rows, send_edges, finish = swap_halos(
         nx, ny, rim_ref, land_ref, send_sem, recv_sem
     )
     enter()
-    ready()
-    send_rows()
+
+    def first():
+        ready()
+        send_rows()
+
+    prep_kernel(rows, f_ref, c_ref, v_ref, lat_ref, lon_ref, rim_ref, edge_ref, first)
     send_edges()
-    if extra:
-        for k in range(3):
-            outs[k][...] = ins[k][...].T
-        for k in range(3, 5):
-            outs[k][...] = jnp.broadcast_to(ins[k][...], outs[k].shape[::-1]).T
-        slots, lit_ref = ins[5], outs[5]
-        shape = (slots.shape[1], lit_ref.shape[2])
-        slot_rows = refs[3]
-        slot_rows[...] = jnp.broadcast_to(slots[...], shape[::-1]).T
-
-        def mark(r, carry):
-            hit = slot_rows[...] == lanes_of(shape) + r * shape[1]
-            lit_ref[r] = jnp.max(jnp.where(hit, 1.0, 0.0), axis=0, keepdims=True)
-            return carry
-
-        lax.fori_loop(0, lit_ref.shape[0], mark, 0)
+    for k in range(3):
+        outs[k][...] = ins[k][...].T
+    for k in range(3, 5):
+        outs[k][...] = jnp.broadcast_to(ins[k][...], outs[k].shape[::-1]).T
+    slots, lit_ref = ins[5], outs[5]
+    shape = (slots.shape[1], lit_ref.shape[2])
+    slot_rows[...] = jnp.broadcast_to(slots[...], shape[::-1]).T
+
+    def mark(r, carry):
+        hit = slot_rows[...] == lanes_of(shape) + r * shape[1]
+        lit_ref[r] = jnp.max(jnp.where(hit, 1.0, 0.0), axis=0, keepdims=True)
+        return carry
+
+    lax.fori_loop(0, lit_ref.shape[0], mark, 0)
 
     finish()
     for k in range(4):
         halo_ref[k] = land_ref[k].astype(jnp.float32)
 
 
-def exchange(rim, number, ins, shapes):
-    _, depth, cols = rim.shape
+def exchange(fields, courant, ins, shapes):
+    count, levels, rows, cols = fields.shape
+    total = count * levels
+    depth = total + levels
     nx, ny = lax.axis_size("gx"), lax.axis_size("gy")
+    f32 = jnp.float32
     return pl.pallas_call(
-        functools.partial(exchange_kernel, len(ins), nx, ny),
-        out_shape=(jax.ShapeDtypeStruct((4, depth, cols), jnp.float32), *shapes),
-        in_specs=[VMEM] * (1 + len(ins)),
-        out_specs=(VMEM,) * (1 + len(shapes)),
+        functools.partial(exchange_kernel, rows, nx, ny),
+        out_shape=(
+            jax.ShapeDtypeStruct((4, depth, cols), f32),
+            jax.ShapeDtypeStruct((rows, total, cols), f32),
+            jax.ShapeDtypeStruct((rows, levels, cols), f32),
+            jax.ShapeDtypeStruct((rows, levels, cols), f32),
+            *shapes,
+        ),
+        in_specs=[VMEM] * (2 + len(ins)),
+        out_specs=(VMEM,) * (4 + len(shapes)),
         scratch_shapes=[
+            pltpu.VMEM((3, depth, cols), jnp.bfloat16),
+            pltpu.VMEM((depth, cols), f32),
             pltpu.VMEM((4, depth, cols), jnp.bfloat16),
             pltpu.SemaphoreType.DMA((4,)),
             pltpu.SemaphoreType.DMA((4,)),
-        ]
-        + ([pltpu.VMEM((ins[5].shape[1], cols), jnp.int32)] if ins else []),
-        compiler_params=pltpu.CompilerParams(collective_id=number, has_side_effects=True),
-        name="exchange%d" % number,
-    )(rim, *ins)
+            pltpu.VMEM((ins[5].shape[1], cols), jnp.int32),
+        ],
+        compiler_params=pltpu.CompilerParams(collective_id=0, has_side_effects=True),
+        name="exchange",
+    )(
+        fields.reshape(total * rows, cols),
+        courant.reshape(2 * levels * rows, cols),
+        *ins,
+    )
 
 
 def step_kernel(
@@ -593,7 +590,6 @@
 ):
     field_count, levels, rows, cols = fields.shape
     columns = rows * cols
-    v, lat, lon, rim = prep(fields, courant)
     place = lax.axis_index("gx")
     flags = jnp.stack([place > 0, place < lax.axis_size("gx") - 1]).astype(jnp.float32)
     bf16, f32 = jnp.bfloat16, jnp.float32
@@ -610,7 +606,7 @@
         *(jax.ShapeDtypeStruct((b.shape[1], cols), f32) for b in ins[3:5]),
         jax.ShapeDtypeStruct((rows, 1, cols), f32),
     )
-    chalo, w1, w2, w3, b1, b2, lit = exchange(rim, 0, ins, shapes)
+    chalo, v, lat, lon, w1, w2, w3, b1, b2, lit = exchange(fields, courant, ins, shapes)
     nets = (w1, b1, w2, b2, w3)
 
     segment_count = columns // SEG

time: 154 us -> 149 us (0.968)
  the two profiles are of different devices: /device:TPU:25 before, /device:TPU:29 now
where the time goes in v5:
time: 149 us
  Pallas kernels  142 us (95%)
  other arithmetic  3.5 us (2%)
  local copies, waits for them, and re-layouts  2.98 us (2%)
    pallas_call x1, Pallas kernels, route(): pl.pallas_call(functools.partial(route_kernel, lax.axis_size('gy'), 8), o...  60.5 us
    pallas_call x2, Pallas kernels, step(): pl.pallas_call(functools.partial(step_kernel, last, lax.axis_size('gx'),...  51 us
    pallas_call x1, Pallas kernels, exchange(): pl.pallas_call(functools.partial(exchange_kernel, rows, nx, ny), out_shap...  20.7 us
    pallas_call x1, Pallas kernels, chem(): pl.pallas_call(chem_kernel, grid=(blocks // per,), out_shape=jax.ShapeDty...  9.65 us

profile of v5, /device:TPU:29, one launch (start us, length us, event | category | flops | bytes accessed | tf_op | source)
XLA Modules:
  0.0 149.1 jit_solution(1606017676399046761)
XLA Ops:
  0.6 20.7 %exchange.1 = (f32[4,640,128]{2,1,0:T(8,128)}, f32[16,512,128]{2,1,0:T(8,128)}, f32[16,128,128]{2,1,0:T(8,128)}, f32[16,128,128]{2,1,0:T(8,128)}, bf16[1024,512]...) custom-call(f32[8192,128]{1,0:T(8,128)} %bitcast.14, ...), custom_call_target="tpu_custom_call" | custom-call | tf_op jit(solution)/shard_map/exchange/pallas_call | solution.py:181
  21.4 0.6 add_convert_fusion.flag_ref
  22.0 27.8 %step_first.1 = (f32[16,512,128]{2,1,0:T(8,128)}, f32[4,512,128]{2,1,0:T(8,128)}) custom-call(f32[2]{0:T(128)} %add_convert_fusion.flag_ref, f32[16,512,128]{2,1,0:T(8,128)} %get-tuple-element.18.v_ref, f32[16,128,128]{2,1,0:T(8,128)} %get-tuple-element.19.lat_ref, f32[16,128,128]{2,1,0:T(8,128)} %get-tuple-element.20.lon_ref, ...), custom_call_target="tpu_custom_call" | custom-call | tf_op jit(solution)/shard_map/step_first/pallas_call | solution.py:381
  49.8 0.0 copy-start
  49.9 23.1 %step_last.1 = (f32[8192,128]{1,0:T(8,128)}, bf16[256,2048]{1,0:T(8,128)(2,1)}) custom-call(f32[2]{0:T(128)} %add_convert_fusion.flag_ref, f32[16,512,128]{2,1,0:T(8,128)} %get-tuple-element.28.v_ref, f32[16,128,128]{2,1,0:T(8,128)} %get-tuple-element.19.lat_ref, f32[16,128,128]{2,1,0:T(8,128)} %get-tuple-element.20.lon_ref, ...), custom_call_target="tpu_custom_call" | custom-call | tf_op jit(solution)/shard_map/step_last/pallas_call | solution.py:381
  73.0 0.0 copy-done
  73.0 0.5 convert_reduce_fusion
  73.5 0.9 select_reduce_fusion
  74.5 0.7 sub.7.tag_ref
  75.2 0.2 broadcast_in_dim.19
  75.4 0.9 reshape_reshape.3.target_ref
  76.3 60.5 %route.1 = (bf16[32,64,512]{2,1,0:T(8,128)(2,1)}, s32[32,1,64]{2,1,0:T(1,128)}) custom-call(bf16[256,2048]{1,0:T(8,128)(2,1)} %get-tuple-element.31.source_ref, s32[1,2048]{1,0:T(1,128)} %reshape_reshape.3.target_ref, s32[32,1,64]{2,1,0:T(1,128)} %sub.7.tag_ref), custom_call_target="tpu_custom_call" | custom-call | tf_op jit(solution)/shard_map/route/pallas_call | solution.py:505
  136.8 0.5 broadcast.28
  137.3 1.4 reduce.3
  138.7 0.7 reshape.73.tag_ref
  139.4 9.7 %chem.1 = bf16[2048,256]{1,0:T(8,128)(2,1)} custom-call(bf16[2048,512]{1,0:T(8,128)(2,1)} %bitcast.16, s32[1,2048]{1,0:T(1,128)} %reshape.73.tag_ref, bf16[16,128,128]{2,1,0:T(8,128)(2,1)} %bitcast.18, bf16[256,1024]{1,0:T(8,128)(2,1)} %w1_ref.1, f32[1,1024]{1,0:T(1,128)} %bitcast.25, bf16[1024,256]{1,0:T(8,128)(2,1)} %w2_ref.1), custom_call_target="tpu_custom_call" | custom-call | tf_op jit(solution)/shard_map/chem/pallas_call | solution.py:558
  (3 shorter events, 0.0 us)
Async XLA Ops:
  49.8 23.2 %copy-start = (s32[2,1,1,1024]{3,2,1,0:T(1,128)S(1)}, s32[2,1,1,1024]{3,2,1,0:T(1,128)}, u32[]{:S(2)}) copy-start(s32[2,1,1,1024]{3,2,1,0:T(1,128)} %param.21) | copy-start | bytes 24580
